TPU v7x, 256 devices: a whole 4x4x8 slice. The times are simulated.
256 devices in a mesh: tile: 32 (over z_lo, y, core), head: 8 (over x, z_hi).
Axes of the slice: x: 4, y: 4, z: 8 (z_hi: 2, z_lo: 4; z = z_hi * 4 + z_lo), core: 2. Of those that a mesh axis runs over, the one named last changes fastest.
Arguments:
- queries: bfloat16 [8192, 5120], P('tile', 'head'), may hold values from -5 to 5
- keys: bfloat16 [8192, 5120], P('tile', 'head'), may hold values from -12 to 12
- values: bfloat16 [8192, 5120], P('tile', 'head'), may hold values from -6 to 6
- reward_grad: bfloat16 [8192, 5120], P('tile', 'head'), may hold values from -6 to 6
- window_mask: int32 [32, 27], replicated, may hold values from 0 to 1, as said below
Outputs:
- attended: bfloat16 [8192, 5120], P('tile', 'head')
- grad_queries: bfloat16 [8192, 5120], P('tile', 'head')
- grad_keys: bfloat16 [8192, 5120], P('tile', 'head')
- grad_values: bfloat16 [8192, 5120], P('tile', 'head')
Inputs may be any that keep to these rules, and one draw needn't show every extreme that they name: `window_mask`: entry (a, 13), the tile itself, is always 1; offsets that leave the grid are always 0.
All inputs are finite; a program needn't handle non-finite values.
Results may differ from a plain program's by a relative error of at most 0.01.
Values may be sent and summed in bfloat16 or wider, within the bound.
A program may use at most 128 MiB of HBM per device.

v0:
```python
import math

import jax
import jax.numpy as jnp
from jax import lax
from jax.sharding import PartitionSpec as P

HD = 128
GH = 4
GW = 2


def swapped(block, axis, apart):
    count = lax.axis_size(axis)
    route = []
    for low in range(count):
        high = low | 1 << apart
        if high != low and high < count:
            route += [(low, high), (high, low)]
    return lax.ppermute(block, axis, route)


def from_behind(value, axis, steps):
    count = lax.axis_size(axis)
    initial, last = (max(0, -steps), min(count, count - steps))
    return lax.ppermute(value, axis, [(source, source + steps) for source in range(initial, last)])


def score_rows(left, right, factor):
    return (
        lax.dot_general(left, right, (((1,), (1,)), ((), ())), preferred_element_type=jnp.float32)
        * factor
    )


def window_fetch(stacked, column, precise):
    per_frame = GH * GW
    if precise:
        partner = swapped(stacked, "tile", 0)
    else:
        partner = swapped(stacked, "tile", 0)
    first = column == 0
    paired = jnp.stack([jnp.where(first, stacked, partner), jnp.where(first, partner, stacked)])
    blocks = []
    for step_t in (-1, 0, 1):
        for step_h in (-1, 0, 1):
            reach = step_t * per_frame + step_h * GW
            if reach == 0:
                blocks.append(paired)
            elif precise:
                blocks.append(from_behind(paired, "tile", -reach))
            else:
                blocks.append(from_behind(paired, "tile", -reach))
    gathered = jnp.stack(blocks)
    return gathered.reshape((18,) + stacked.shape)


def on_device(queries, keys, values, reward_grad, window_mask):
    tok, width = queries.shape
    heads_here = width // HD
    per_frame = GH * GW
    tiles_all = lax.axis_size("tile")
    frames = tiles_all // per_frame
    myself = lax.axis_index("tile")
    frame = myself // per_frame
    row = myself // GW % GH
    column = myself % GW
    slots = jnp.arange(18, dtype=jnp.int32)
    step_t = slots // 6 - 1
    step_h = slots // 2 % 3 - 1
    across = slots % 2
    near_t = frame + step_t
    near_h = row + step_h
    inside = (near_t >= 0) & (near_t < frames) & (near_h >= 0) & (near_h < GH)
    own_mask = lax.dynamic_index_in_dim(window_mask, myself, 0, keepdims=False)
    ahead = (step_t + 1) * 9 + (step_h + 1) * 3 + across - column + 1
    valid_out = inside & (own_mask[ahead] == 1)
    sources = jnp.clip(near_t * per_frame + near_h * GW + across, 0, tiles_all - 1)
    behind = (1 - step_t) * 9 + (1 - step_h) * 3 + column - across + 1
    valid_in = inside & (window_mask[sources, behind] == 1)
    key_live = jnp.repeat(valid_out, tok)
    query_live = jnp.repeat(valid_in, tok)
    scale = 1.0 / math.sqrt(HD)

    def columns(array, start):
        return lax.dynamic_slice_in_dim(array, start, HD, array.ndim - 1)

    def forward_head(index, carry):
        outputs, grads, stats = carry
        start = index * HD
        query = columns(queries, start)
        grad_here = columns(reward_grad, start)
        fetched = window_fetch(
            jnp.stack([columns(keys, start), columns(values, start)]), column, False
        )
        near_keys = fetched[:, 0].reshape(18 * tok, HD)
        near_values = fetched[:, 1].reshape(18 * tok, HD)
        scores = score_rows(query, near_keys, scale)
        masked = jnp.where(key_live[None, :], scores, -jnp.inf)
        top = jnp.max(masked, axis=1)
        logsum = top + jnp.log(jnp.sum(jnp.exp(masked - top[:, None]), axis=1))
        weights = jnp.exp(masked - logsum[:, None])
        probs = weights.astype(jnp.bfloat16)
        output = jnp.dot(probs, near_values, preferred_element_type=jnp.float32).astype(
            jnp.bfloat16
        )
        delta = jnp.sum(grad_here.astype(jnp.float32) * output.astype(jnp.float32), axis=1)
        dprob = score_rows(grad_here, near_values, 1.0)
        dscore = (weights * (dprob - delta[:, None]) * scale).astype(jnp.bfloat16)
        grad_query = jnp.dot(dscore, near_keys, preferred_element_type=jnp.float32).astype(
            jnp.bfloat16
        )
        outputs = lax.dynamic_update_slice_in_dim(outputs, output, start, 1)
        grads = lax.dynamic_update_slice_in_dim(grads, grad_query, start, 1)
        stats = lax.dynamic_update_index_in_dim(stats, jnp.stack([logsum, delta]), index, 0)
        return (outputs, grads, stats)

    blank = jnp.zeros((tok, width), jnp.bfloat16)
    stat_blank = jnp.zeros((heads_here, 2, tok), jnp.float32)
    attended, grad_queries, stats = lax.fori_loop(
        0, heads_here, forward_head, (blank, blank, stat_blank)
    )

    def backward_head(index, carry):
        key_out, value_out = carry
        start = index * HD
        key_here = columns(keys, start)
        value_here = columns(values, start)
        incoming = window_fetch(
            jnp.stack([columns(queries, start), columns(reward_grad, start)]), column, False
        )
        numbers = window_fetch(
            lax.dynamic_index_in_dim(stats, index, 0, keepdims=False), column, True
        )
        near_queries = incoming[:, 0].reshape(18 * tok, HD)
        near_grads = incoming[:, 1].reshape(18 * tok, HD)
        near_logsum = numbers[:, 0].reshape(18 * tok)
        near_delta = numbers[:, 1].reshape(18 * tok)
        scores = score_rows(near_queries, key_here, scale)
        shifted = jnp.where(query_live[:, None], scores - near_logsum[:, None], -jnp.inf)
        weights = jnp.exp(shifted)
        probs = weights.astype(jnp.bfloat16)
        dprob = score_rows(near_grads, value_here, 1.0)
        dscore = (weights * (dprob - near_delta[:, None]) * scale).astype(jnp.bfloat16)
        grad_key = lax.dot_general(
            dscore, near_queries, (((0,), (0,)), ((), ())), preferred_element_type=jnp.float32
        )
        grad_value = lax.dot_general(
            probs, near_grads, (((0,), (0,)), ((), ())), preferred_element_type=jnp.float32
        )
        key_out = lax.dynamic_update_slice_in_dim(key_out, grad_key.astype(jnp.bfloat16), start, 1)
        value_out = lax.dynamic_update_slice_in_dim(
            value_out, grad_value.astype(jnp.bfloat16), start, 1
        )
        return (key_out, value_out)

    grad_keys, grad_values = lax.fori_loop(0, heads_here, backward_head, (blank, blank))
    return (attended, grad_queries, grad_keys, grad_values)


def solution(mesh):
    return jax.shard_map(
        on_device,
        mesh=mesh,
        in_specs=(P("tile", "head"), P("tile", "head"), P("tile", "head"), P("tile", "head"), P()),
        out_specs=(P("tile", "head"), P("tile", "head"), P("tile", "head"), P("tile", "head")),
        check_vma=False,
    )
```

profile of v0, /device:TPU:56, one launch (start us, length us, event | category | flops | bytes accessed | tf_op | source)
XLA Modules:
  0.0 697.8 jit_solution(52107849301928112)
XLA Ops:
  3.0 267.2 %while.38 = (s32[]{:T(128)}, bf16[256,640]{1,0:T(8,128)(2,1)S(1)}, bf16[256,640]{1,0:T(8,128)(2,1)S(1)}, f32[5,2,256]{2,1,0:T(2,128)S(1)}, bf16[256,640]{1,0:T(8...) while((s32[]{:T(128)}, bf16[256,640]{1,0:T(8,128)(2,1)S(1)}, ...), condition=%wide.region_4.5_spmd.clone, body=%wide.region_0.4_spmd.clone.sunk | while | flops 1223229440 | bytes 63276644 | solution.py:120
  5.4 4.8 collective-permute-start.1
  27.0 4.7 collective-permute-start.4
  35.4 6.2 collective-permute-done.4
  41.7 7.1 %collective-permute-done.5 = bf16[2,2,256,128]{3,2,1,0:T(8,128)(2,1)S(1)} collective-permute-done((bf16[2,2,256,128]{3,2,1,0:T(8,128)(2,1)S(1)}, bf16[2,2,256,128]{3,2,1,0:T(8,128)(2,1)S(1)}, u32[]{:S(2)}, u32[]{:S(2)}) %collective-permute-start.5) | collective-permute-done | bytes 262176 | tf_op jit(solution)/shard_map/while/body/eval_jaxpr/ppermute | solution.py:26
  91.6 10.1 %collective-permute-done.5 = bf16[2,2,256,128]{3,2,1,0:T(8,128)(2,1)S(1)} collective-permute-done((bf16[2,2,256,128]{3,2,1,0:T(8,128)(2,1)S(1)}, bf16[2,2,256,128]{3,2,1,0:T(8,128)(2,1)S(1)}, u32[]{:S(2)}, u32[]{:S(2)}) %collective-permute-start.5) | collective-permute-done | bytes 262176 | tf_op jit(solution)/shard_map/while/body/eval_jaxpr/ppermute | solution.py:26
  144.5 10.1 %collective-permute-done.5 = bf16[2,2,256,128]{3,2,1,0:T(8,128)(2,1)S(1)} collective-permute-done((bf16[2,2,256,128]{3,2,1,0:T(8,128)(2,1)S(1)}, bf16[2,2,256,128]{3,2,1,0:T(8,128)(2,1)S(1)}, u32[]{:S(2)}, u32[]{:S(2)}) %collective-permute-start.5) | collective-permute-done | bytes 262176 | tf_op jit(solution)/shard_map/while/body/eval_jaxpr/ppermute | solution.py:26
  197.5 10.1 %collective-permute-done.5 = bf16[2,2,256,128]{3,2,1,0:T(8,128)(2,1)S(1)} collective-permute-done((bf16[2,2,256,128]{3,2,1,0:T(8,128)(2,1)S(1)}, bf16[2,2,256,128]{3,2,1,0:T(8,128)(2,1)S(1)}, u32[]{:S(2)}, u32[]{:S(2)}) %collective-permute-start.5) | collective-permute-done | bytes 262176 | tf_op jit(solution)/shard_map/while/body/eval_jaxpr/ppermute | solution.py:26
  250.4 10.1 %collective-permute-done.5 = bf16[2,2,256,128]{3,2,1,0:T(8,128)(2,1)S(1)} collective-permute-done((bf16[2,2,256,128]{3,2,1,0:T(8,128)(2,1)S(1)}, bf16[2,2,256,128]{3,2,1,0:T(8,128)(2,1)S(1)}, u32[]{:S(2)}, u32[]{:S(2)}) %collective-permute-start.5) | collective-permute-done | bytes 262176 | tf_op jit(solution)/shard_map/while/body/eval_jaxpr/ppermute | solution.py:26
  271.2 425.9 %while.39 = (s32[]{:T(128)}, bf16[256,640]{1,0:T(8,128)(2,1)}, bf16[256,640]{1,0:T(8,128)(2,1)S(1)}, pred[]{:T(512)}, bf16[256,640]{1,0:T(8,128)(2,1)}, /*index=...) while((s32[]{:T(128)}, bf16[256,640]{1,0:T(8,128)(2,1)}, ...), condition=%wide.region_6.7_spmd.clone, body=%wide.region_5.6_spmd.clone.sunk | while | flops 1218382848 | bytes 58372036 | solution.py:157
  274.8 4.6 collective-permute-start.26
  288.8 4.8 collective-permute-start.21
  303.8 4.8 collective-permute-done.23
  308.7 4.7 collective-permute-start.10
  323.6 4.8 collective-permute-start.12
  328.4 5.5 collective-permute-start.13
  337.9 8.5 %collective-permute-done.14 = bf16[2,2,256,128]{3,2,1,0:T(8,128)(2,1)S(1)} collective-permute-done((bf16[2,2,256,128]{3,2,1,0:T(8,128)(2,1)S(1)}, bf16[2,2,256,128]{3,2,1,0:T(8,128)(2,1)S(1)}, u32[]{:S(2)}, u32[]{:S(2)}) %collective-permute-start.14) | collective-permute-done | bytes 262176 | tf_op jit(solution)/shard_map/while/body/eval_jaxpr/ppermute | solution.py:26
  351.2 5.2 fusion.105
  360.0 4.6 collective-permute-start.26
  373.9 4.8 collective-permute-start.21
  389.0 4.8 collective-permute-done.23
  393.8 4.7 collective-permute-start.10
  408.8 4.8 collective-permute-start.12
  413.6 5.5 collective-permute-start.13
  423.1 8.5 %collective-permute-done.14 = bf16[2,2,256,128]{3,2,1,0:T(8,128)(2,1)S(1)} collective-permute-done((bf16[2,2,256,128]{3,2,1,0:T(8,128)(2,1)S(1)}, bf16[2,2,256,128]{3,2,1,0:T(8,128)(2,1)S(1)}, u32[]{:S(2)}, u32[]{:S(2)}) %collective-permute-start.14) | collective-permute-done | bytes 262176 | tf_op jit(solution)/shard_map/while/body/eval_jaxpr/ppermute | solution.py:26
  436.4 5.2 fusion.105
  459.1 4.8 collective-permute-start.21
  474.1 4.8 collective-permute-done.23
  479.0 4.7 collective-permute-start.10
  493.9 4.8 collective-permute-start.12
  498.8 5.5 collective-permute-start.13
  508.3 8.5 %collective-permute-done.14 = bf16[2,2,256,128]{3,2,1,0:T(8,128)(2,1)S(1)} collective-permute-done((bf16[2,2,256,128]{3,2,1,0:T(8,128)(2,1)S(1)}, bf16[2,2,256,128]{3,2,1,0:T(8,128)(2,1)S(1)}, u32[]{:S(2)}, u32[]{:S(2)}) %collective-permute-start.14) | collective-permute-done | bytes 262176 | tf_op jit(solution)/shard_map/while/body/eval_jaxpr/ppermute | solution.py:26
  521.5 5.2 fusion.105
  544.3 4.8 collective-permute-start.21
  559.3 4.8 collective-permute-done.23
  564.2 4.7 collective-permute-start.10
  579.1 4.8 collective-permute-start.12
  584.0 5.5 collective-permute-start.13
  593.4 8.5 %collective-permute-done.14 = bf16[2,2,256,128]{3,2,1,0:T(8,128)(2,1)S(1)} collective-permute-done((bf16[2,2,256,128]{3,2,1,0:T(8,128)(2,1)S(1)}, bf16[2,2,256,128]{3,2,1,0:T(8,128)(2,1)S(1)}, u32[]{:S(2)}, u32[]{:S(2)}) %collective-permute-start.14) | collective-permute-done | bytes 262176 | tf_op jit(solution)/shard_map/while/body/eval_jaxpr/ppermute | solution.py:26
  606.7 5.2 fusion.105
  615.5 4.6 collective-permute-start.26
  629.5 4.8 collective-permute-start.21
  644.5 4.8 collective-permute-done.23
  649.4 4.7 collective-permute-start.10
  664.3 4.8 collective-permute-start.12
  669.1 5.5 collective-permute-start.13
  678.6 8.5 %collective-permute-done.14 = bf16[2,2,256,128]{3,2,1,0:T(8,128)(2,1)S(1)} collective-permute-done((bf16[2,2,256,128]{3,2,1,0:T(8,128)(2,1)S(1)}, bf16[2,2,256,128]{3,2,1,0:T(8,128)(2,1)S(1)}, u32[]{:S(2)}, u32[]{:S(2)}) %collective-permute-start.14) | collective-permute-done | bytes 262176 | tf_op jit(solution)/shard_map/while/body/eval_jaxpr/ppermute | solution.py:26
  691.9 5.2 fusion.105
  (564 shorter events, 425.0 us)
Async XLA Ops:
  13.3 35.6 %collective-permute-start.8 = (bf16[2,2,256,128]{3,2,1,0:T(8,128)(2,1)S(1)}, bf16[2,2,256,128]{3,2,1,0:T(8,128)(2,1)S(1)}, u32[]{:S(2)}, u32[]{:S(2)}) collective-permute-start(bf16[2,2,256,128]{3,2,1,0:T(8,128)(2,1)S(1)} %pad_maximum_fusion.11), channel_id=1, source_target_pairs={{80,0},{88,8},{96,16},{104,24},{112,32},{120,40},{128,48},{136,56}... | collective-permute-start | bytes 786440 | tf_op jit(solution)/shard_map/while/body/eval_jaxpr/ppermute | solution.py:26
  17.1 31.8 %collective-permute-start.7 = (bf16[2,2,256,128]{3,2,1,0:T(8,128)(2,1)S(1)}, bf16[2,2,256,128]{3,2,1,0:T(8,128)(2,1)S(1)}, u32[]{:S(2)}, u32[]{:S(2)}) collective-permute-start(bf16[2,2,256,128]{3,2,1,0:T(8,128)(2,1)S(1)} %pad_maximum_fusion.11), channel_id=1, source_target_pairs={{64,0},{72,8},{80,16},{88,24},{96,32},{104,40},{112,48},{120,56},{... | collective-permute-start | bytes 786440 | tf_op jit(solution)/shard_map/while/body/eval_jaxpr/ppermute | solution.py:26
  19.0 29.8 %collective-permute-start.6 = (bf16[2,2,256,128]{3,2,1,0:T(8,128)(2,1)S(1)}, bf16[2,2,256,128]{3,2,1,0:T(8,128)(2,1)S(1)}, u32[]{:S(2)}, u32[]{:S(2)}) collective-permute-start(bf16[2,2,256,128]{3,2,1,0:T(8,128)(2,1)S(1)} %pad_maximum_fusion.11), channel_id=1, source_target_pairs={{48,0},{56,8},{64,16},{72,24},{80,32},{88,40},{96,48},{104,56},{11... | collective-permute-start | bytes 786440 | tf_op jit(solution)/shard_map/while/body/eval_jaxpr/ppermute | solution.py:26
  65.9 35.9 %collective-permute-start.8 = (bf16[2,2,256,128]{3,2,1,0:T(8,128)(2,1)S(1)}, bf16[2,2,256,128]{3,2,1,0:T(8,128)(2,1)S(1)}, u32[]{:S(2)}, u32[]{:S(2)}) collective-permute-start(bf16[2,2,256,128]{3,2,1,0:T(8,128)(2,1)S(1)} %pad_maximum_fusion.11), channel_id=1, source_target_pairs={{80,0},{88,8},{96,16},{104,24},{112,32},{120,40},{128,48},{136,56}... | collective-permute-start | bytes 786440 | tf_op jit(solution)/shard_map/while/body/eval_jaxpr/ppermute | solution.py:26
  70.1 31.7 %collective-permute-start.7 = (bf16[2,2,256,128]{3,2,1,0:T(8,128)(2,1)S(1)}, bf16[2,2,256,128]{3,2,1,0:T(8,128)(2,1)S(1)}, u32[]{:S(2)}, u32[]{:S(2)}) collective-permute-start(bf16[2,2,256,128]{3,2,1,0:T(8,128)(2,1)S(1)} %pad_maximum_fusion.11), channel_id=1, source_target_pairs={{64,0},{72,8},{80,16},{88,24},{96,32},{104,40},{112,48},{120,56},{... | collective-permute-start | bytes 786440 | tf_op jit(solution)/shard_map/while/body/eval_jaxpr/ppermute | solution.py:26
  72.1 29.7 %collective-permute-start.6 = (bf16[2,2,256,128]{3,2,1,0:T(8,128)(2,1)S(1)}, bf16[2,2,256,128]{3,2,1,0:T(8,128)(2,1)S(1)}, u32[]{:S(2)}, u32[]{:S(2)}) collective-permute-start(bf16[2,2,256,128]{3,2,1,0:T(8,128)(2,1)S(1)} %pad_maximum_fusion.11), channel_id=1, source_target_pairs={{48,0},{56,8},{64,16},{72,24},{80,32},{88,40},{96,48},{104,56},{11... | collective-permute-start | bytes 786440 | tf_op jit(solution)/shard_map/while/body/eval_jaxpr/ppermute | solution.py:26
  118.8 35.9 %collective-permute-start.8 = (bf16[2,2,256,128]{3,2,1,0:T(8,128)(2,1)S(1)}, bf16[2,2,256,128]{3,2,1,0:T(8,128)(2,1)S(1)}, u32[]{:S(2)}, u32[]{:S(2)}) collective-permute-start(bf16[2,2,256,128]{3,2,1,0:T(8,128)(2,1)S(1)} %pad_maximum_fusion.11), channel_id=1, source_target_pairs={{80,0},{88,8},{96,16},{104,24},{112,32},{120,40},{128,48},{136,56}... | collective-permute-start | bytes 786440 | tf_op jit(solution)/shard_map/while/body/eval_jaxpr/ppermute | solution.py:26
  123.1 31.6 %collective-permute-start.7 = (bf16[2,2,256,128]{3,2,1,0:T(8,128)(2,1)S(1)}, bf16[2,2,256,128]{3,2,1,0:T(8,128)(2,1)S(1)}, u32[]{:S(2)}, u32[]{:S(2)}) collective-permute-start(bf16[2,2,256,128]{3,2,1,0:T(8,128)(2,1)S(1)} %pad_maximum_fusion.11), channel_id=1, source_target_pairs={{64,0},{72,8},{80,16},{88,24},{96,32},{104,40},{112,48},{120,56},{... | collective-permute-start | bytes 786440 | tf_op jit(solution)/shard_map/while/body/eval_jaxpr/ppermute | solution.py:26
  125.0 29.7 %collective-permute-start.6 = (bf16[2,2,256,128]{3,2,1,0:T(8,128)(2,1)S(1)}, bf16[2,2,256,128]{3,2,1,0:T(8,128)(2,1)S(1)}, u32[]{:S(2)}, u32[]{:S(2)}) collective-permute-start(bf16[2,2,256,128]{3,2,1,0:T(8,128)(2,1)S(1)} %pad_maximum_fusion.11), channel_id=1, source_target_pairs={{48,0},{56,8},{64,16},{72,24},{80,32},{88,40},{96,48},{104,56},{11... | collective-permute-start | bytes 786440 | tf_op jit(solution)/shard_map/while/body/eval_jaxpr/ppermute | solution.py:26
  171.8 35.9 %collective-permute-start.8 = (bf16[2,2,256,128]{3,2,1,0:T(8,128)(2,1)S(1)}, bf16[2,2,256,128]{3,2,1,0:T(8,128)(2,1)S(1)}, u32[]{:S(2)}, u32[]{:S(2)}) collective-permute-start(bf16[2,2,256,128]{3,2,1,0:T(8,128)(2,1)S(1)} %pad_maximum_fusion.11), channel_id=1, source_target_pairs={{80,0},{88,8},{96,16},{104,24},{112,32},{120,40},{128,48},{136,56}... | collective-permute-start | bytes 786440 | tf_op jit(solution)/shard_map/while/body/eval_jaxpr/ppermute | solution.py:26
  176.0 31.6 %collective-permute-start.7 = (bf16[2,2,256,128]{3,2,1,0:T(8,128)(2,1)S(1)}, bf16[2,2,256,128]{3,2,1,0:T(8,128)(2,1)S(1)}, u32[]{:S(2)}, u32[]{:S(2)}) collective-permute-start(bf16[2,2,256,128]{3,2,1,0:T(8,128)(2,1)S(1)} %pad_maximum_fusion.11), channel_id=1, source_target_pairs={{64,0},{72,8},{80,16},{88,24},{96,32},{104,40},{112,48},{120,56},{... | collective-permute-start | bytes 786440 | tf_op jit(solution)/shard_map/while/body/eval_jaxpr/ppermute | solution.py:26
  177.9 29.7 %collective-permute-start.6 = (bf16[2,2,256,128]{3,2,1,0:T(8,128)(2,1)S(1)}, bf16[2,2,256,128]{3,2,1,0:T(8,128)(2,1)S(1)}, u32[]{:S(2)}, u32[]{:S(2)}) collective-permute-start(bf16[2,2,256,128]{3,2,1,0:T(8,128)(2,1)S(1)} %pad_maximum_fusion.11), channel_id=1, source_target_pairs={{48,0},{56,8},{64,16},{72,24},{80,32},{88,40},{96,48},{104,56},{11... | collective-permute-start | bytes 786440 | tf_op jit(solution)/shard_map/while/body/eval_jaxpr/ppermute | solution.py:26
  224.7 35.9 %collective-permute-start.8 = (bf16[2,2,256,128]{3,2,1,0:T(8,128)(2,1)S(1)}, bf16[2,2,256,128]{3,2,1,0:T(8,128)(2,1)S(1)}, u32[]{:S(2)}, u32[]{:S(2)}) collective-permute-start(bf16[2,2,256,128]{3,2,1,0:T(8,128)(2,1)S(1)} %pad_maximum_fusion.11), channel_id=1, source_target_pairs={{80,0},{88,8},{96,16},{104,24},{112,32},{120,40},{128,48},{136,56}... | collective-permute-start | bytes 786440 | tf_op jit(solution)/shard_map/while/body/eval_jaxpr/ppermute | solution.py:26
  228.9 31.6 %collective-permute-start.7 = (bf16[2,2,256,128]{3,2,1,0:T(8,128)(2,1)S(1)}, bf16[2,2,256,128]{3,2,1,0:T(8,128)(2,1)S(1)}, u32[]{:S(2)}, u32[]{:S(2)}) collective-permute-start(bf16[2,2,256,128]{3,2,1,0:T(8,128)(2,1)S(1)} %pad_maximum_fusion.11), channel_id=1, source_target_pairs={{64,0},{72,8},{80,16},{88,24},{96,32},{104,40},{112,48},{120,56},{... | collective-permute-start | bytes 786440 | tf_op jit(solution)/shard_map/while/body/eval_jaxpr/ppermute | solution.py:26
  230.8 29.7 %collective-permute-start.6 = (bf16[2,2,256,128]{3,2,1,0:T(8,128)(2,1)S(1)}, bf16[2,2,256,128]{3,2,1,0:T(8,128)(2,1)S(1)}, u32[]{:S(2)}, u32[]{:S(2)}) collective-permute-start(bf16[2,2,256,128]{3,2,1,0:T(8,128)(2,1)S(1)} %pad_maximum_fusion.11), channel_id=1, source_target_pairs={{48,0},{56,8},{64,16},{72,24},{80,32},{88,40},{96,48},{104,56},{11... | collective-permute-start | bytes 786440 | tf_op jit(solution)/shard_map/while/body/eval_jaxpr/ppermute | solution.py:26
  274.4 34.2 %collective-permute-start.9 = (bf16[2,256,128]{2,1,0:T(8,128)(2,1)S(1)}, bf16[2,256,128]{2,1,0:T(8,128)(2,1)S(1)}, u32[]{:S(2)}, u32[]{:S(2)}) collective-permute-start(bf16[2,256,128]{2,1,0:T(8,128)(2,1)S(1)} %pad_maximum_fusion.12), channel_id=1, source_target_pairs={{0,8},{8,0},{16,24},{24,16},{32,40},{40,32},{48,56},{56,48},{64,72... | collective-permute-start | bytes 393224 | tf_op jit(solution)/shard_map/while/body/eval_jaxpr/ppermute | solution.py:20
  274.8 38.6 %collective-permute-start.26 = (f32[2,2,256]{2,1,0:T(2,128)S(1)}, f32[2,2,256]{2,1,0:T(2,128)S(1)}, u32[]{:S(2)}, u32[]{:S(2)}) collective-permute-start(f32[2,2,256]{2,1,0:T(2,128)S(1)} %pad_maximum_fusion.14), channel_id=1, source_target_pairs={{80,0},{88,8},{96,16},{104,24},{112,32},{120,40},{128,48},{136,56}... | collective-permute-start | bytes 12296 | tf_op jit(solution)/shard_map/while/body/eval_jaxpr/ppermute | solution.py:26
  279.4 29.2 %collective-permute-start.25 = (f32[2,2,256]{2,1,0:T(2,128)S(1)}, f32[2,2,256]{2,1,0:T(2,128)S(1)}, u32[]{:S(2)}, u32[]{:S(2)}) collective-permute-start(f32[2,2,256]{2,1,0:T(2,128)S(1)} %pad_maximum_fusion.14), channel_id=1, source_target_pairs={{64,0},{72,8},{80,16},{88,24},{96,32},{104,40},{112,48},{120,56},{... | collective-permute-start | bytes 12296 | tf_op jit(solution)/shard_map/while/body/eval_jaxpr/ppermute | solution.py:26
  281.3 27.2 %collective-permute-start.24 = (f32[2,2,256]{2,1,0:T(2,128)S(1)}, f32[2,2,256]{2,1,0:T(2,128)S(1)}, u32[]{:S(2)}, u32[]{:S(2)}) collective-permute-start(f32[2,2,256]{2,1,0:T(2,128)S(1)} %pad_maximum_fusion.14), channel_id=1, source_target_pairs={{48,0},{56,8},{64,16},{72,24},{80,32},{88,40},{96,48},{104,56},{11... | collective-permute-start | bytes 12296 | tf_op jit(solution)/shard_map/while/body/eval_jaxpr/ppermute | solution.py:26
  315.5 31.1 %collective-permute-start.17 = (bf16[2,2,256,128]{3,2,1,0:T(8,128)(2,1)S(1)}, bf16[2,2,256,128]{3,2,1,0:T(8,128)(2,1)S(1)}, u32[]{:S(2)}, u32[]{:S(2)}) collective-permute-start(bf16[2,2,256,128]{3,2,1,0:T(8,128)(2,1)S(1)} %pad_maximum_fusion.13), channel_id=1, source_target_pairs={{80,0},{88,8},{96,16},{104,24},{112,32},{120,40},{128,48},{136,56}... | collective-permute-start | bytes 786440 | tf_op jit(solution)/shard_map/while/body/eval_jaxpr/ppermute | solution.py:26
  319.7 26.9 %collective-permute-start.16 = (bf16[2,2,256,128]{3,2,1,0:T(8,128)(2,1)S(1)}, bf16[2,2,256,128]{3,2,1,0:T(8,128)(2,1)S(1)}, u32[]{:S(2)}, u32[]{:S(2)}) collective-permute-start(bf16[2,2,256,128]{3,2,1,0:T(8,128)(2,1)S(1)} %pad_maximum_fusion.13), channel_id=1, source_target_pairs={{64,0},{72,8},{80,16},{88,24},{96,32},{104,40},{112,48},{120,56},{... | collective-permute-start | bytes 786440 | tf_op jit(solution)/shard_map/while/body/eval_jaxpr/ppermute | solution.py:26
  359.6 34.2 %collective-permute-start.9 = (bf16[2,256,128]{2,1,0:T(8,128)(2,1)S(1)}, bf16[2,256,128]{2,1,0:T(8,128)(2,1)S(1)}, u32[]{:S(2)}, u32[]{:S(2)}) collective-permute-start(bf16[2,256,128]{2,1,0:T(8,128)(2,1)S(1)} %pad_maximum_fusion.12), channel_id=1, source_target_pairs={{0,8},{8,0},{16,24},{24,16},{32,40},{40,32},{48,56},{56,48},{64,72... | collective-permute-start | bytes 393224 | tf_op jit(solution)/shard_map/while/body/eval_jaxpr/ppermute | solution.py:20
  360.0 38.6 %collective-permute-start.26 = (f32[2,2,256]{2,1,0:T(2,128)S(1)}, f32[2,2,256]{2,1,0:T(2,128)S(1)}, u32[]{:S(2)}, u32[]{:S(2)}) collective-permute-start(f32[2,2,256]{2,1,0:T(2,128)S(1)} %pad_maximum_fusion.14), channel_id=1, source_target_pairs={{80,0},{88,8},{96,16},{104,24},{112,32},{120,40},{128,48},{136,56}... | collective-permute-start | bytes 12296 | tf_op jit(solution)/shard_map/while/body/eval_jaxpr/ppermute | solution.py:26
  364.6 29.2 %collective-permute-start.25 = (f32[2,2,256]{2,1,0:T(2,128)S(1)}, f32[2,2,256]{2,1,0:T(2,128)S(1)}, u32[]{:S(2)}, u32[]{:S(2)}) collective-permute-start(f32[2,2,256]{2,1,0:T(2,128)S(1)} %pad_maximum_fusion.14), channel_id=1, source_target_pairs={{64,0},{72,8},{80,16},{88,24},{96,32},{104,40},{112,48},{120,56},{... | collective-permute-start | bytes 12296 | tf_op jit(solution)/shard_map/while/body/eval_jaxpr/ppermute | solution.py:26
  366.5 27.2 %collective-permute-start.24 = (f32[2,2,256]{2,1,0:T(2,128)S(1)}, f32[2,2,256]{2,1,0:T(2,128)S(1)}, u32[]{:S(2)}, u32[]{:S(2)}) collective-permute-start(f32[2,2,256]{2,1,0:T(2,128)S(1)} %pad_maximum_fusion.14), channel_id=1, source_target_pairs={{48,0},{56,8},{64,16},{72,24},{80,32},{88,40},{96,48},{104,56},{11... | collective-permute-start | bytes 12296 | tf_op jit(solution)/shard_map/while/body/eval_jaxpr/ppermute | solution.py:26
  400.7 31.1 %collective-permute-start.17 = (bf16[2,2,256,128]{3,2,1,0:T(8,128)(2,1)S(1)}, bf16[2,2,256,128]{3,2,1,0:T(8,128)(2,1)S(1)}, u32[]{:S(2)}, u32[]{:S(2)}) collective-permute-start(bf16[2,2,256,128]{3,2,1,0:T(8,128)(2,1)S(1)} %pad_maximum_fusion.13), channel_id=1, source_target_pairs={{80,0},{88,8},{96,16},{104,24},{112,32},{120,40},{128,48},{136,56}... | collective-permute-start | bytes 786440 | tf_op jit(solution)/shard_map/while/body/eval_jaxpr/ppermute | solution.py:26
  404.9 26.9 %collective-permute-start.16 = (bf16[2,2,256,128]{3,2,1,0:T(8,128)(2,1)S(1)}, bf16[2,2,256,128]{3,2,1,0:T(8,128)(2,1)S(1)}, u32[]{:S(2)}, u32[]{:S(2)}) collective-permute-start(bf16[2,2,256,128]{3,2,1,0:T(8,128)(2,1)S(1)} %pad_maximum_fusion.13), channel_id=1, source_target_pairs={{64,0},{72,8},{80,16},{88,24},{96,32},{104,40},{112,48},{120,56},{... | collective-permute-start | bytes 786440 | tf_op jit(solution)/shard_map/while/body/eval_jaxpr/ppermute | solution.py:26
  406.8 24.9 %collective-permute-start.15 = (bf16[2,2,256,128]{3,2,1,0:T(8,128)(2,1)S(1)}, bf16[2,2,256,128]{3,2,1,0:T(8,128)(2,1)S(1)}, u32[]{:S(2)}, u32[]{:S(2)}) collective-permute-start(bf16[2,2,256,128]{3,2,1,0:T(8,128)(2,1)S(1)} %pad_maximum_fusion.13), channel_id=1, source_target_pairs={{48,0},{56,8},{64,16},{72,24},{80,32},{88,40},{96,48},{104,56},{11... | collective-permute-start | bytes 786440 | tf_op jit(solution)/shard_map/while/body/eval_jaxpr/ppermute | solution.py:26
  444.7 34.2 %collective-permute-start.9 = (bf16[2,256,128]{2,1,0:T(8,128)(2,1)S(1)}, bf16[2,256,128]{2,1,0:T(8,128)(2,1)S(1)}, u32[]{:S(2)}, u32[]{:S(2)}) collective-permute-start(bf16[2,256,128]{2,1,0:T(8,128)(2,1)S(1)} %pad_maximum_fusion.12), channel_id=1, source_target_pairs={{0,8},{8,0},{16,24},{24,16},{32,40},{40,32},{48,56},{56,48},{64,72... | collective-permute-start | bytes 393224 | tf_op jit(solution)/shard_map/while/body/eval_jaxpr/ppermute | solution.py:20
  445.2 38.6 %collective-permute-start.26 = (f32[2,2,256]{2,1,0:T(2,128)S(1)}, f32[2,2,256]{2,1,0:T(2,128)S(1)}, u32[]{:S(2)}, u32[]{:S(2)}) collective-permute-start(f32[2,2,256]{2,1,0:T(2,128)S(1)} %pad_maximum_fusion.14), channel_id=1, source_target_pairs={{80,0},{88,8},{96,16},{104,24},{112,32},{120,40},{128,48},{136,56}... | collective-permute-start | bytes 12296 | tf_op jit(solution)/shard_map/while/body/eval_jaxpr/ppermute | solution.py:26
  449.7 29.2 %collective-permute-start.25 = (f32[2,2,256]{2,1,0:T(2,128)S(1)}, f32[2,2,256]{2,1,0:T(2,128)S(1)}, u32[]{:S(2)}, u32[]{:S(2)}) collective-permute-start(f32[2,2,256]{2,1,0:T(2,128)S(1)} %pad_maximum_fusion.14), channel_id=1, source_target_pairs={{64,0},{72,8},{80,16},{88,24},{96,32},{104,40},{112,48},{120,56},{... | collective-permute-start | bytes 12296 | tf_op jit(solution)/shard_map/while/body/eval_jaxpr/ppermute | solution.py:26
  451.7 27.2 %collective-permute-start.24 = (f32[2,2,256]{2,1,0:T(2,128)S(1)}, f32[2,2,256]{2,1,0:T(2,128)S(1)}, u32[]{:S(2)}, u32[]{:S(2)}) collective-permute-start(f32[2,2,256]{2,1,0:T(2,128)S(1)} %pad_maximum_fusion.14), channel_id=1, source_target_pairs={{48,0},{56,8},{64,16},{72,24},{80,32},{88,40},{96,48},{104,56},{11... | collective-permute-start | bytes 12296 | tf_op jit(solution)/shard_map/while/body/eval_jaxpr/ppermute | solution.py:26
  485.8 31.1 %collective-permute-start.17 = (bf16[2,2,256,128]{3,2,1,0:T(8,128)(2,1)S(1)}, bf16[2,2,256,128]{3,2,1,0:T(8,128)(2,1)S(1)}, u32[]{:S(2)}, u32[]{:S(2)}) collective-permute-start(bf16[2,2,256,128]{3,2,1,0:T(8,128)(2,1)S(1)} %pad_maximum_fusion.13), channel_id=1, source_target_pairs={{80,0},{88,8},{96,16},{104,24},{112,32},{120,40},{128,48},{136,56}... | collective-permute-start | bytes 786440 | tf_op jit(solution)/shard_map/while/body/eval_jaxpr/ppermute | solution.py:26
  490.1 26.9 %collective-permute-start.16 = (bf16[2,2,256,128]{3,2,1,0:T(8,128)(2,1)S(1)}, bf16[2,2,256,128]{3,2,1,0:T(8,128)(2,1)S(1)}, u32[]{:S(2)}, u32[]{:S(2)}) collective-permute-start(bf16[2,2,256,128]{3,2,1,0:T(8,128)(2,1)S(1)} %pad_maximum_fusion.13), channel_id=1, source_target_pairs={{64,0},{72,8},{80,16},{88,24},{96,32},{104,40},{112,48},{120,56},{... | collective-permute-start | bytes 786440 | tf_op jit(solution)/shard_map/while/body/eval_jaxpr/ppermute | solution.py:26
  492.0 24.9 %collective-permute-start.15 = (bf16[2,2,256,128]{3,2,1,0:T(8,128)(2,1)S(1)}, bf16[2,2,256,128]{3,2,1,0:T(8,128)(2,1)S(1)}, u32[]{:S(2)}, u32[]{:S(2)}) collective-permute-start(bf16[2,2,256,128]{3,2,1,0:T(8,128)(2,1)S(1)} %pad_maximum_fusion.13), channel_id=1, source_target_pairs={{48,0},{56,8},{64,16},{72,24},{80,32},{88,40},{96,48},{104,56},{11... | collective-permute-start | bytes 786440 | tf_op jit(solution)/shard_map/while/body/eval_jaxpr/ppermute | solution.py:26
  529.9 34.2 %collective-permute-start.9 = (bf16[2,256,128]{2,1,0:T(8,128)(2,1)S(1)}, bf16[2,256,128]{2,1,0:T(8,128)(2,1)S(1)}, u32[]{:S(2)}, u32[]{:S(2)}) collective-permute-start(bf16[2,256,128]{2,1,0:T(8,128)(2,1)S(1)} %pad_maximum_fusion.12), channel_id=1, source_target_pairs={{0,8},{8,0},{16,24},{24,16},{32,40},{40,32},{48,56},{56,48},{64,72... | collective-permute-start | bytes 393224 | tf_op jit(solution)/shard_map/while/body/eval_jaxpr/ppermute | solution.py:20
  530.3 38.6 %collective-permute-start.26 = (f32[2,2,256]{2,1,0:T(2,128)S(1)}, f32[2,2,256]{2,1,0:T(2,128)S(1)}, u32[]{:S(2)}, u32[]{:S(2)}) collective-permute-start(f32[2,2,256]{2,1,0:T(2,128)S(1)} %pad_maximum_fusion.14), channel_id=1, source_target_pairs={{80,0},{88,8},{96,16},{104,24},{112,32},{120,40},{128,48},{136,56}... | collective-permute-start | bytes 12296 | tf_op jit(solution)/shard_map/while/body/eval_jaxpr/ppermute | solution.py:26
  534.9 29.2 %collective-permute-start.25 = (f32[2,2,256]{2,1,0:T(2,128)S(1)}, f32[2,2,256]{2,1,0:T(2,128)S(1)}, u32[]{:S(2)}, u32[]{:S(2)}) collective-permute-start(f32[2,2,256]{2,1,0:T(2,128)S(1)} %pad_maximum_fusion.14), channel_id=1, source_target_pairs={{64,0},{72,8},{80,16},{88,24},{96,32},{104,40},{112,48},{120,56},{... | collective-permute-start | bytes 12296 | tf_op jit(solution)/shard_map/while/body/eval_jaxpr/ppermute | solution.py:26
  536.9 27.2 %collective-permute-start.24 = (f32[2,2,256]{2,1,0:T(2,128)S(1)}, f32[2,2,256]{2,1,0:T(2,128)S(1)}, u32[]{:S(2)}, u32[]{:S(2)}) collective-permute-start(f32[2,2,256]{2,1,0:T(2,128)S(1)} %pad_maximum_fusion.14), channel_id=1, source_target_pairs={{48,0},{56,8},{64,16},{72,24},{80,32},{88,40},{96,48},{104,56},{11... | collective-permute-start | bytes 12296 | tf_op jit(solution)/shard_map/while/body/eval_jaxpr/ppermute | solution.py:26
  571.0 31.1 %collective-permute-start.17 = (bf16[2,2,256,128]{3,2,1,0:T(8,128)(2,1)S(1)}, bf16[2,2,256,128]{3,2,1,0:T(8,128)(2,1)S(1)}, u32[]{:S(2)}, u32[]{:S(2)}) collective-permute-start(bf16[2,2,256,128]{3,2,1,0:T(8,128)(2,1)S(1)} %pad_maximum_fusion.13), channel_id=1, source_target_pairs={{80,0},{88,8},{96,16},{104,24},{112,32},{120,40},{128,48},{136,56}... | collective-permute-start | bytes 786440 | tf_op jit(solution)/shard_map/while/body/eval_jaxpr/ppermute | solution.py:26
  575.2 26.9 %collective-permute-start.16 = (bf16[2,2,256,128]{3,2,1,0:T(8,128)(2,1)S(1)}, bf16[2,2,256,128]{3,2,1,0:T(8,128)(2,1)S(1)}, u32[]{:S(2)}, u32[]{:S(2)}) collective-permute-start(bf16[2,2,256,128]{3,2,1,0:T(8,128)(2,1)S(1)} %pad_maximum_fusion.13), channel_id=1, source_target_pairs={{64,0},{72,8},{80,16},{88,24},{96,32},{104,40},{112,48},{120,56},{... | collective-permute-start | bytes 786440 | tf_op jit(solution)/shard_map/while/body/eval_jaxpr/ppermute | solution.py:26
  615.1 34.2 %collective-permute-start.9 = (bf16[2,256,128]{2,1,0:T(8,128)(2,1)S(1)}, bf16[2,256,128]{2,1,0:T(8,128)(2,1)S(1)}, u32[]{:S(2)}, u32[]{:S(2)}) collective-permute-start(bf16[2,256,128]{2,1,0:T(8,128)(2,1)S(1)} %pad_maximum_fusion.12), channel_id=1, source_target_pairs={{0,8},{8,0},{16,24},{24,16},{32,40},{40,32},{48,56},{56,48},{64,72... | collective-permute-start | bytes 393224 | tf_op jit(solution)/shard_map/while/body/eval_jaxpr/ppermute | solution.py:20
  615.5 38.6 %collective-permute-start.26 = (f32[2,2,256]{2,1,0:T(2,128)S(1)}, f32[2,2,256]{2,1,0:T(2,128)S(1)}, u32[]{:S(2)}, u32[]{:S(2)}) collective-permute-start(f32[2,2,256]{2,1,0:T(2,128)S(1)} %pad_maximum_fusion.14), channel_id=1, source_target_pairs={{80,0},{88,8},{96,16},{104,24},{112,32},{120,40},{128,48},{136,56}... | collective-permute-start | bytes 12296 | tf_op jit(solution)/shard_map/while/body/eval_jaxpr/ppermute | solution.py:26
  620.1 29.2 %collective-permute-start.25 = (f32[2,2,256]{2,1,0:T(2,128)S(1)}, f32[2,2,256]{2,1,0:T(2,128)S(1)}, u32[]{:S(2)}, u32[]{:S(2)}) collective-permute-start(f32[2,2,256]{2,1,0:T(2,128)S(1)} %pad_maximum_fusion.14), channel_id=1, source_target_pairs={{64,0},{72,8},{80,16},{88,24},{96,32},{104,40},{112,48},{120,56},{... | collective-permute-start | bytes 12296 | tf_op jit(solution)/shard_map/while/body/eval_jaxpr/ppermute | solution.py:26
  622.0 27.2 %collective-permute-start.24 = (f32[2,2,256]{2,1,0:T(2,128)S(1)}, f32[2,2,256]{2,1,0:T(2,128)S(1)}, u32[]{:S(2)}, u32[]{:S(2)}) collective-permute-start(f32[2,2,256]{2,1,0:T(2,128)S(1)} %pad_maximum_fusion.14), channel_id=1, source_target_pairs={{48,0},{56,8},{64,16},{72,24},{80,32},{88,40},{96,48},{104,56},{11... | collective-permute-start | bytes 12296 | tf_op jit(solution)/shard_map/while/body/eval_jaxpr/ppermute | solution.py:26
  656.2 31.1 %collective-permute-start.17 = (bf16[2,2,256,128]{3,2,1,0:T(8,128)(2,1)S(1)}, bf16[2,2,256,128]{3,2,1,0:T(8,128)(2,1)S(1)}, u32[]{:S(2)}, u32[]{:S(2)}) collective-permute-start(bf16[2,2,256,128]{3,2,1,0:T(8,128)(2,1)S(1)} %pad_maximum_fusion.13), channel_id=1, source_target_pairs={{80,0},{88,8},{96,16},{104,24},{112,32},{120,40},{128,48},{136,56}... | collective-permute-start | bytes 786440 | tf_op jit(solution)/shard_map/while/body/eval_jaxpr/ppermute | solution.py:26
  660.4 26.9 %collective-permute-start.16 = (bf16[2,2,256,128]{3,2,1,0:T(8,128)(2,1)S(1)}, bf16[2,2,256,128]{3,2,1,0:T(8,128)(2,1)S(1)}, u32[]{:S(2)}, u32[]{:S(2)}) collective-permute-start(bf16[2,2,256,128]{3,2,1,0:T(8,128)(2,1)S(1)} %pad_maximum_fusion.13), channel_id=1, source_target_pairs={{64,0},{72,8},{80,16},{88,24},{96,32},{104,40},{112,48},{120,56},{... | collective-permute-start | bytes 786440 | tf_op jit(solution)/shard_map/while/body/eval_jaxpr/ppermute | solution.py:26
  662.3 24.9 %collective-permute-start.15 = (bf16[2,2,256,128]{3,2,1,0:T(8,128)(2,1)S(1)}, bf16[2,2,256,128]{3,2,1,0:T(8,128)(2,1)S(1)}, u32[]{:S(2)}, u32[]{:S(2)}) collective-permute-start(bf16[2,2,256,128]{3,2,1,0:T(8,128)(2,1)S(1)} %pad_maximum_fusion.13), channel_id=1, source_target_pairs={{48,0},{56,8},{64,16},{72,24},{80,32},{88,40},{96,48},{104,56},{11... | collective-permute-start | bytes 786440 | tf_op jit(solution)/shard_map/while/body/eval_jaxpr/ppermute | solution.py:26
  (101 other events, 930.9 us)
where the time goes:
time: 703 us; the launch traced here: 698 us
  starting transfers between devices  376 us (53%)
  waiting for transfers between devices  198 us (28%)
  matrix products  77 us (11%)
  local copies, waits for them, and re-layouts  37.3 us (5%)
    ppermute x120, starting transfers between devices, from_behind(): lax.ppermute(value, axis, [(source, source + steps) for source in range(i...  374 us
    ppermute x120, waiting for transfers between devices, from_behind(): lax.ppermute(value, axis, [(source, source + steps) for source in range(i...  190 us
    dot_general x5, matrix products, backward_head(): lax.dot_general(dscore, near_queries, (((0,), (0,)), ((), ())), preferred...  26.2 us
    dot_general x5, matrix products, forward_head(): jnp.dot(dscore, near_keys, preferred_element_type=jnp.float32)  21.3 us
    dot_general x10, matrix products, score_rows(): lax.dot_general(left, right, (((1,), (1,)), ((), ())), preferred_element_...  19.6 us
    while x125, local copies, waits for them, and re-layouts  15.8 us
  transfers between devices with their start and end apart: 135, of which 70 were waited for; matrix products, arithmetic and copies ran while one was open for 2% of the time, Pallas kernels for 0%

commit v1 on v0

v1 whole, which is shorter than its diff:
```python
import functools
import math

import jax
import jax.numpy as jnp
from jax import lax
from jax.experimental import pallas as pl
from jax.experimental.pallas import tpu as pltpu
from jax.sharding import PartitionSpec as P

HD = 128
GH = 4
GW = 2


QD_LO, QD_HI, KV_LO, KV_HI, KVP = 0, 1, 2, 3, 4
ST_LO, ST_HI, FIN_LO, FIN_HI, OQ_LO, OQ_HI, DKV, DZ_LO, DZ_HI = 7, 8, 9, 10, 11, 12, 13, 14, 15
KINDS = 16

NT = (((1,), (1,)), ((), ()))
NEG = -1e30
BIG = 3e30
MESH = pl.DeviceIdType.MESH


def mm(left, right, dims=(((1,), (0,)), ((), ()))):
    return lax.dot_general(left, right, dims, preferred_element_type=jnp.float32)


def kernel(
    heads,
    tok,
    frames,
    mask_ref,
    q_hbm,
    k_hbm,
    v_hbm,
    g_hbm,
    att_ref,
    gq_ref,
    gk_ref,
    gv_ref,
    qd,
    kv,
    kvt,
    scores,
    ef,
    ovk,
    wt,
    st,
    stin,
    fin,
    oq_out,
    oq_in,
    dkv_own,
    dkv_out,
    dkv_in,
    dz_out,
    dz_in,
    load_sem,
    send_sem,
    recv_sem,
):
    me = lax.axis_index("tile")
    per_frame = GH * GW
    frame = me // per_frame
    row = me // GW % GH
    column = me % GW
    partner = me + 1 - 2 * column
    has_ym, has_yp = row > 0, row < GH - 1
    has_zm, has_zp = frame > 0, frame < frames - 1
    ym, yp, zm, zp = me - GW, me + GW, me - per_frame, me + per_frame
    scale = 1.0 / math.sqrt(HD)
    scale2 = scale * math.log2(math.e)
    bf16, f32 = jnp.bfloat16, jnp.float32

    def rows(slot):
        return pl.ds(slot * tok, tok)

    def table(kind, j):
        if kind in (QD_LO, QD_HI):
            low = kind == QD_LO
            return (
                qd.at[j, rows(1), :],
                qd.at[j, rows(0 if low else 2), :],
                yp if low else ym,
                has_yp if low else has_ym,
                has_ym if low else has_yp,
            )
        if kind in (KV_LO, KV_HI):
            low = kind == KV_LO
            return (
                kv.at[j, rows(1), :],
                kv.at[j, rows(0 if low else 2), :],
                zp if low else zm,
                has_zp if low else has_zm,
                has_zm if low else has_zp,
            )
        if kind in (KVP, KVP + 1, KVP + 2):
            d = kind - KVP
            there = (has_zm, None, has_zp)[d]
            return (kv.at[j, rows(d), :], kv.at[j, rows(3 + d), :], partner, there, there)
        if kind == DKV:
            return (dkv_out.at[j], dkv_in.at[j], partner, None, None)
        if kind in (DZ_LO, DZ_HI):
            low = kind == DZ_LO
            return (
                dz_out.at[j, 1 if low else 0],
                dz_in.at[j, 0 if low else 1],
                zp if low else zm,
                has_zp if low else has_zm,
                has_zm if low else has_zp,
            )
        low = kind in (ST_LO, FIN_LO, OQ_LO)
        if kind in (ST_LO, ST_HI):
            source, target = st.at[j, 2 if low else 0], stin.at[j, 0 if low else 1]
        elif kind in (FIN_LO, FIN_HI):
            source, target = fin.at[j, 1], fin.at[j, 0 if low else 2]
        else:
            source, target = oq_out.at[j, 1 if low else 0], oq_in.at[j, 0 if low else 1]
        return (
            source,
            target,
            yp if low else ym,
            has_yp if low else has_ym,
            has_ym if low else has_yp,
        )

    def copy_of(kind, j):
        source, target, device, sent, received = table(kind, j)
        copy = pltpu.make_async_remote_copy(
            src_ref=source,
            dst_ref=target,
            send_sem=send_sem.at[kind, j],
            recv_sem=recv_sem.at[kind, j],
            device_id={"tile": device},
            device_id_type=MESH,
        )
        return copy, sent, received

    def guarded(condition, action):
        if condition is None:
            action()
        else:
            pl.when(condition)(action)

    def send(kind, j):
        copy, sent, _ = copy_of(kind, j)
        guarded(sent, copy.start)

    def arrive(kind, j):
        copy, _, received = copy_of(kind, j)
        guarded(received, copy.wait_recv)

    def sent_off(kind, j):
        copy, sent, _ = copy_of(kind, j)
        guarded(sent, copy.wait_send)

    def start_load(j, _):
        start = pl.multiple_of(j * HD, HD)
        for which, ref, buffer, lane in (
            (0, g_hbm, qd, 0),
            (0, q_hbm, qd, HD),
            (1, v_hbm, kv, 0),
            (1, k_hbm, kv, HD),
        ):
            pltpu.make_async_copy(
                ref.at[:, pl.ds(start, HD)],
                buffer.at[j, rows(1), pl.ds(lane, HD)],
                load_sem.at[which, j],
            ).start()
        return 0

    lax.fori_loop(0, heads, start_load, 0)

    def blank(j, _):
        for missing, slot in ((row == 0, 0), (row == GH - 1, 2)):
            @pl.when(missing)
            def _():
                side = slot // 2
                qd[j, rows(slot), :] = jnp.zeros((tok, 2 * HD), bf16)
                stin[j, side] = jnp.concatenate(
                    [jnp.full((1, tok), NEG, f32), jnp.zeros((7, tok), f32)], axis=0
                )
                fin[j, slot] = jnp.zeros((8, tok), f32)
                oq_in[j, side] = jnp.zeros((2 * HD, tok), bf16)

        for missing, slot in ((frame == 0, 0), (frame == frames - 1, 2)):
            @pl.when(missing)
            def _():
                kv[j, rows(slot), :] = jnp.zeros((tok, 2 * HD), bf16)
                kv[j, rows(3 + slot), :] = jnp.zeros((tok, 2 * HD), bf16)
                dz_in[j, slot // 2] = jnp.zeros((tok, 2 * HD), bf16)

        return 0

    barrier = pltpu.get_barrier_semaphore()

    def greet(device):
        pl.semaphore_signal(barrier, inc=1, device_id={"tile": device}, device_id_type=MESH)

    greet(partner)
    for there, device in ((has_ym, ym), (has_yp, yp), (has_zm, zm), (has_zp, zp)):
        pl.when(there)(functools.partial(greet, device))
    lax.fori_loop(0, heads, blank, 0)
    peers = sum(jnp.where(there, 1, 0) for there in (has_ym, has_yp, has_zm, has_zp))
    pl.semaphore_wait(barrier, 1 + peers)

    def send_own(j, _):
        for which, buffer in ((1, kv), (0, qd)):
            own = buffer.at[j, rows(1), :]
            pltpu.make_async_copy(own, own, load_sem.at[which, j]).wait()
            for kind in ((KV_LO, KV_HI, KVP + 1), (QD_LO, QD_HI))[1 - which]:
                send(kind, j)
        return 0

    lax.fori_loop(0, heads, send_own, 0)

    def relay(j):
        for kind, onward in ((KV_LO, KVP), (KV_HI, KVP + 2)):
            arrive(kind, j)
            send(onward, j)

    relay(0)

    def prepare(j):
        for kind in (KVP, KVP + 1, KVP + 2, QD_LO, QD_HI):
            arrive(kind, j)
        for kt in range(6):
            kvt[:, rows(kt)] = kv[j, rows(kt), :].T

    def forward(j, s):
        ring = lax.rem(j, 2)
        qrows = pl.ds(pl.multiple_of(s * tok, tok), tok)
        tile = me + (s - 1) * GW
        near = row + s - 1
        exists = jnp.where((near >= 0) & (near < GH), 1, 0)
        tile = jnp.where(exists == 1, tile, me)
        drops = []
        for kt in range(6):
            across = 1 if kt < 3 else 2 - 2 * column
            flag = mask_ref[tile, kt % 3 * 9 + (2 - s) * 3 + across] * exists
            drops.append((1 - flag).astype(f32))
        query = qd[j, qrows, HD:]
        grad = qd[j, qrows, :HD]
        top = jnp.full((1, tok), NEG, f32)
        for kt in range(6):
            block = mm(kv[j, rows(kt), HD:], query, NT) * scale2
            scores[rows(kt), :] = block
            top = jnp.maximum(top, jnp.max(block, axis=0, keepdims=True) + drops[kt] * NEG)
        total = jnp.zeros((1, tok), f32)
        moment = jnp.zeros((1, tok), f32)
        ecols = pl.ds(pl.multiple_of(s * 2 * tok, tok), tok)
        fcols = pl.ds(pl.multiple_of((s * 2 + 1) * tok, tok), tok)
        for kt in range(6):
            weight = jnp.exp2(scores[rows(kt), :] - (top + drops[kt] * BIG))
            slope = weight * mm(kv[j, rows(kt), :HD], grad, NT)
            total += jnp.sum(weight, axis=0, keepdims=True)
            moment += jnp.sum(slope, axis=0, keepdims=True)
            ef[ring, rows(kt), ecols] = weight.astype(bf16)
            ef[ring, rows(kt), fcols] = slope.astype(bf16)
        ovk[j, s, : 2 * HD, :] = mm(kvt[...], ef[ring, :, ecols])
        ovk[j, s, 2 * HD :, :] = mm(kvt[HD:, :], ef[ring, :, fcols])
        st[j, s, 0:1, :] = top
        st[j, s, 1:2, :] = total
        st[j, s, 2:3, :] = moment

    def combine(j):
        arrive(ST_LO, j)
        arrive(ST_HI, j)
        parts = (stin.at[j, 0], st.at[j, 1], stin.at[j, 1])
        tops = [part[0:1, :] for part in parts]
        top = jnp.maximum(jnp.maximum(tops[0], tops[1]), tops[2])
        shares = [jnp.exp2(one - top) for one in tops]
        total = sum(share * part[1:2, :] for share, part in zip(shares, parts))
        moment = sum(share * part[2:3, :] for share, part in zip(shares, parts))
        inverse = 1.0 / total
        fin[j, 1, 0:1, :] = top
        fin[j, 1, 1:2, :] = inverse
        fin[j, 1, 2:3, :] = moment * inverse
        send(FIN_LO, j)
        send(FIN_HI, j)

    def backward(j):
        ring = lax.rem(j, 2)
        arrive(FIN_LO, j)
        arrive(FIN_HI, j)
        for s in (0, 2, 1):
            share = jnp.exp2(st[j, s, 0:1, :] - fin[j, s, 0:1, :]) * fin[j, s, 1:2, :]
            delta = fin[j, s, 2:3, :]
            scaled = share * scale
            output = ovk[j, s, :HD, :] * share
            grad_query = (ovk[j, s, 2 * HD :, :] - delta * ovk[j, s, HD : 2 * HD, :]) * scaled
            if s == 1:
                ovk[j, s, :HD, :] = output
                ovk[j, s, HD : 2 * HD, :] = grad_query
            else:
                oq_out[j, s // 2, :HD, :] = output.astype(bf16)
                oq_out[j, s // 2, HD:, :] = grad_query.astype(bf16)
                send(OQ_HI if s == 0 else OQ_LO, j)
            flipped = qd[j, rows(s), :].astype(f32).T
            ecols = pl.ds(s * 2 * tok, tok)
            fcols = pl.ds((s * 2 + 1) * tok, tok)
            wt[:HD, ecols] = (flipped[:HD] * share).astype(bf16)
            wt[HD:, ecols] = (flipped[HD:] * (-scaled * delta)).astype(bf16)
            wt[:HD, fcols] = jnp.zeros((HD, tok), bf16)
            wt[HD:, fcols] = (flipped[HD:] * scaled).astype(bf16)
        for kt in (3, 4, 5, 0, 1, 2):
            part = mm(ef[ring, rows(kt), :], wt[...], NT)
            if kt < 3:
                dkv_own[j, kt] = part
            else:
                dkv_out[j, kt - 3] = part.astype(bf16)
            if kt == 5:
                send(DKV, j)

    def hand_back(j):
        arrive(DKV, j)
        for d, kind in ((0, DZ_HI), (2, DZ_LO)):
            dz_out[j, d // 2] = (dkv_own[j, d] + dkv_in[j, d].astype(f32)).astype(bf16)
            send(kind, j)

    def finish(j):
        for kind in (OQ_LO, OQ_HI, DZ_LO, DZ_HI):
            arrive(kind, j)
        cols = pl.ds(pl.multiple_of(j * HD, HD), HD)
        both = ovk[j, 1, : 2 * HD, :] + oq_in[j, 0].astype(f32) + oq_in[j, 1].astype(f32)
        both = both.T
        att_ref[:, cols] = both[:, :HD].astype(bf16)
        gq_ref[:, cols] = both[:, HD:].astype(bf16)
        both = dkv_own[j, 1] + dkv_in[j, 1].astype(f32)
        both = both + dz_in[j, 0].astype(f32) + dz_in[j, 1].astype(f32)
        gv_ref[:, cols] = both[:, :HD].astype(bf16)
        gk_ref[:, cols] = both[:, HD:].astype(bf16)

    def step(i, _):
        @pl.when(i < heads)
        def _():
            prepare(i)

        def inner(s, _):
            @pl.when(i < heads)
            def _():
                forward(i, s)

                @pl.when(s == 0)
                def _():
                    send(ST_HI, i)

                @pl.when(s == 2)
                def _():
                    send(ST_LO, i)

            @pl.when((s == 0) & (i + 1 < heads))
            def _():
                relay(i + 1)

            @pl.when((s == 0) & (i >= 1) & (i <= heads))
            def _():
                combine(i - 1)

            @pl.when((s == 1) & (i >= 2))
            def _():
                hand_back(i - 2)

            return 0

        lax.fori_loop(0, 3, inner, 0)

        @pl.when((i >= 1) & (i <= heads))
        def _():
            backward(i - 1)

        @pl.when(i >= 2)
        def _():
            finish(i - 2)

        return 0

    lax.fori_loop(0, heads + 2, step, 0)

    def drain(j, _):
        for kind in range(KINDS):
            sent_off(kind, j)
        return 0

    lax.fori_loop(0, heads, drain, 0)


def on_device(queries, keys, values, reward_grad, window_mask):
    tok, width = queries.shape
    heads = width // HD
    frames = lax.axis_size("tile") // (GH * GW)
    bf16, f32 = jnp.bfloat16, jnp.float32
    hbm = pl.BlockSpec(memory_space=pl.ANY)
    vmem = pl.BlockSpec(memory_space=pltpu.VMEM)
    return pl.pallas_call(
        functools.partial(kernel, heads, tok, frames),
        out_shape=[jax.ShapeDtypeStruct((tok, width), bf16)] * 4,
        in_specs=[pl.BlockSpec(memory_space=pltpu.SMEM), hbm, hbm, hbm, hbm],
        out_specs=[vmem] * 4,
        scratch_shapes=[
            pltpu.VMEM((heads, 3 * tok, 2 * HD), bf16),
            pltpu.VMEM((heads, 6 * tok, 2 * HD), bf16),
            pltpu.VMEM((2 * HD, 6 * tok), bf16),
            pltpu.VMEM((6 * tok, tok), f32),
            pltpu.VMEM((2, 6 * tok, 6 * tok), bf16),
            pltpu.VMEM((heads, 3, 3 * HD, tok), f32),
            pltpu.VMEM((2 * HD, 6 * tok), bf16),
            pltpu.VMEM((heads, 3, 8, tok), f32),
            pltpu.VMEM((heads, 2, 8, tok), f32),
            pltpu.VMEM((heads, 3, 8, tok), f32),
            pltpu.VMEM((heads, 2, 2 * HD, tok), bf16),
            pltpu.VMEM((heads, 2, 2 * HD, tok), bf16),
            pltpu.VMEM((heads, 3, tok, 2 * HD), f32),
            pltpu.VMEM((heads, 3, tok, 2 * HD), bf16),
            pltpu.VMEM((heads, 3, tok, 2 * HD), bf16),
            pltpu.VMEM((heads, 2, tok, 2 * HD), bf16),
            pltpu.VMEM((heads, 2, tok, 2 * HD), bf16),
            pltpu.SemaphoreType.DMA((2, heads)),
            pltpu.SemaphoreType.DMA((KINDS, heads)),
            pltpu.SemaphoreType.DMA((KINDS, heads)),
        ],
        compiler_params=pltpu.CompilerParams(
            collective_id=0, has_side_effects=True, vmem_limit_bytes=60 * 1024 * 1024
        ),
    )(window_mask, queries, keys, values, reward_grad)


def solution(mesh):
    return jax.shard_map(
        on_device,
        mesh=mesh,
        in_specs=(P("tile", "head"), P("tile", "head"), P("tile", "head"), P("tile", "head"), P()),
        out_specs=(P("tile", "head"), P("tile", "head"), P("tile", "head"), P("tile", "head")),
        check_vma=False,
    )
```

time: 703 us -> 71.1 us (0.10)
  the two profiles are of different devices: /device:TPU:56 before, /device:TPU:1 now
where the time goes in v1:
time: 71.1 us; the launch traced here: 70.8 us
  Pallas kernels  65.5 us (92%)
  local copies, waits for them, and re-layouts  4.68 us (7%)
    pallas_call x1, Pallas kernels, on_device(): pl.pallas_call(functools.partial(kernel, heads, tok, frames), out_shape=[...  65.5 us
    unnamed x10, local copies, waits for them, and re-layouts  4.68 us

profile of v1, /device:TPU:1, one launch (start us, length us, event | category | flops | bytes accessed | tf_op | source)
XLA Modules:
  0.0 70.8 jit_solution(17640524737383482182)
XLA Ops:
  0.6 65.5 %shard_map.84 = (bf16[256,640]{1,0:T(8,128)(2,1)}, bf16[256,640]{1,0:T(8,128)(2,1)}, bf16[256,640]{1,0:T(8,128)(2,1)}, bf16[256,640]{1,0:T(8,128)(2,1)}) custom-call(s32[32,27]{1,0:T(8,128)} %mask_ref.1, bf16[256,640]{1,0:T(8,128)(2,1)} %q_hbm.1, bf16[256,640]{1,0:T(8,128)(2,1)} %k_hbm.1, bf16[256,640]{1,0:T(8,128)(2,1)} %v_hbm.1, bf16[256,640]{1,0:T(8,128)(2,1)} %g_hbm.1), custom_call_target="tpu_custom_call" | custom-call | tf_op jit(solution)/shard_map/pallas_call | solution.py:397
  66.1 0.0 copy-start.2
  66.1 1.8 %copy.13 = bf16[256,640]{1,0:T(8,128)(2,1)} copy(bf16[256,640]{1,0:T(8,128)(2,1)} %get-tuple-element.8) | data formatting | bytes 655360
  67.9 0.0 copy-done.2
  67.9 0.0 copy-start.1
  67.9 0.7 %copy.14 = bf16[256,640]{1,0:T(8,128)(2,1)} copy(bf16[256,640]{1,0:T(8,128)(2,1)S(1)} %copy-done.2) | data formatting | bytes 655360
  68.6 0.4 copy-done.1
  69.0 0.0 copy-start
  69.0 0.7 %copy.15 = bf16[256,640]{1,0:T(8,128)(2,1)} copy(bf16[256,640]{1,0:T(8,128)(2,1)S(1)} %copy-done.1) | data formatting | bytes 655360
  69.7 0.4 copy-done
  70.1 0.7 %copy.16 = bf16[256,640]{1,0:T(8,128)(2,1)} copy(bf16[256,640]{1,0:T(8,128)(2,1)S(1)} %copy-done) | data formatting | bytes 655360
Async XLA Ops:
  66.1 1.8 %copy-start.2 = (bf16[256,640]{1,0:T(8,128)(2,1)S(1)}, bf16[256,640]{1,0:T(8,128)(2,1)}, u32[]{:S(2)}) copy-start(bf16[256,640]{1,0:T(8,128)(2,1)} %get-tuple-element.9) | copy-start | bytes 983044
  67.9 1.1 %copy-start.1 = (bf16[256,640]{1,0:T(8,128)(2,1)S(1)}, bf16[256,640]{1,0:T(8,128)(2,1)}, u32[]{:S(2)}) copy-start(bf16[256,640]{1,0:T(8,128)(2,1)} %get-tuple-element.10) | copy-start | bytes 983044
  69.0 1.1 %copy-start = (bf16[256,640]{1,0:T(8,128)(2,1)S(1)}, bf16[256,640]{1,0:T(8,128)(2,1)}, u32[]{:S(2)}) copy-start(bf16[256,640]{1,0:T(8,128)(2,1)} %get-tuple-element.11) | copy-start | bytes 983044

commit v2 on v1

--- a/solution.py
+++ b/solution.py
@@ -15,7 +15,13 @@
 
 QD_LO, QD_HI, KV_LO, KV_HI, KVP = 0, 1, 2, 3, 4
 ST_LO, ST_HI, FIN_LO, FIN_HI, OQ_LO, OQ_HI, DKV, DZ_LO, DZ_HI = 7, 8, 9, 10, 11, 12, 13, 14, 15
-KINDS = 16
+DKV1, DKV2 = 16, 17
+KINDS = 18
+
+AHEAD = 2
+
+ONES = 16
+ESUM = 2 * HD + ONES
 
 NT = (((1,), (1,)), ((), ()))
 NEG = -1e30
@@ -44,6 +50,8 @@
     kv,
     kvt,
     scores,
+    slopes,
+    limits,
     ef,
     ovk,
     wt,
@@ -57,7 +65,9 @@
     dkv_in,
     dz_out,
     dz_in,
+    result,
     load_sem,
+    out_sem,
     send_sem,
     recv_sem,
 ):
@@ -100,8 +110,9 @@
             d = kind - KVP
             there = (has_zm, None, has_zp)[d]
             return (kv.at[j, rows(d), :], kv.at[j, rows(3 + d), :], partner, there, there)
-        if kind == DKV:
-            return (dkv_out.at[j], dkv_in.at[j], partner, None, None)
+        if kind in (DKV, DKV1, DKV2):
+            d = (DKV, DKV1, DKV2).index(kind)
+            return (dkv_out.at[j, d], dkv_in.at[j, d], partner, None, None)
         if kind in (DZ_LO, DZ_HI):
             low = kind == DZ_LO
             return (
@@ -172,6 +183,7 @@
         return 0
 
     lax.fori_loop(0, heads, start_load, 0)
+    kvt[2 * HD :, :] = jnp.ones((ONES, 6 * tok), bf16)
 
     def blank(j, _):
         for missing, slot in ((row == 0, 0), (row == GH - 1, 2)):
@@ -214,7 +226,7 @@
                 send(kind, j)
         return 0
 
-    lax.fori_loop(0, heads, send_own, 0)
+    lax.fori_loop(0, min(AHEAD, heads), send_own, 0)
 
     def relay(j):
         for kind, onward in ((KV_LO, KVP), (KV_HI, KVP + 2)):
@@ -227,7 +239,7 @@
         for kind in (KVP, KVP + 1, KVP + 2, QD_LO, QD_HI):
             arrive(kind, j)
         for kt in range(6):
-            kvt[:, rows(kt)] = kv[j, rows(kt), :].T
+            kvt[: 2 * HD, rows(kt)] = kv[j, rows(kt), :].T
 
     def forward(j, s):
         ring = lax.rem(j, 2)
@@ -245,25 +257,29 @@
         grad = qd[j, qrows, :HD]
         top = jnp.full((1, tok), NEG, f32)
         for kt in range(6):
-            block = mm(kv[j, rows(kt), HD:], query, NT) * scale2
+            block = mm(kv[j, rows(kt), HD:], query, NT)
             scores[rows(kt), :] = block
-            top = jnp.maximum(top, jnp.max(block, axis=0, keepdims=True) + drops[kt] * NEG)
-        total = jnp.zeros((1, tok), f32)
-        moment = jnp.zeros((1, tok), f32)
+            peak = jnp.max(block, axis=0, keepdims=True)
+            top = jnp.maximum(top, peak * scale2 + drops[kt] * NEG)
+            slopes[rows(kt), :] = mm(kv[j, rows(kt), :HD], grad, NT)
+        for kt in range(6):
+            limits[kt : kt + 1, :] = top + drops[kt] * BIG
         ecols = pl.ds(pl.multiple_of(s * 2 * tok, tok), tok)
         fcols = pl.ds(pl.multiple_of((s * 2 + 1) * tok, tok), tok)
-        for kt in range(6):
-            weight = jnp.exp2(scores[rows(kt), :] - (top + drops[kt] * BIG))
-            slope = weight * mm(kv[j, rows(kt), :HD], grad, NT)
-            total += jnp.sum(weight, axis=0, keepdims=True)
-            moment += jnp.sum(slope, axis=0, keepdims=True)
-            ef[ring, rows(kt), ecols] = weight.astype(bf16)
-            ef[ring, rows(kt), fcols] = slope.astype(bf16)
-        ovk[j, s, : 2 * HD, :] = mm(kvt[...], ef[ring, :, ecols])
-        ovk[j, s, 2 * HD :, :] = mm(kvt[HD:, :], ef[ring, :, fcols])
+
+        def weigh(kt, _):
+            krows = pl.ds(pl.multiple_of(kt * tok, tok), tok)
+            weight = jnp.exp2(scores[krows, :] * scale2 - limits[pl.ds(kt, 1), :])
+            ef[ring, krows, ecols] = weight.astype(bf16)
+            ef[ring, krows, fcols] = (weight * slopes[krows, :]).astype(bf16)
+            return 0
+
+        lax.fori_loop(0, 6, weigh, 0)
+        ovk[j, s, :ESUM, :] = mm(kvt[...], ef[ring, :, ecols])
+        ovk[j, s, ESUM:, :] = mm(kvt[HD:, :], ef[ring, :, fcols])
         st[j, s, 0:1, :] = top
-        st[j, s, 1:2, :] = total
-        st[j, s, 2:3, :] = moment
+        st[j, s, 1:2, :] = ovk[j, s, 2 * HD : 2 * HD + 1, :]
+        st[j, s, 2:3, :] = ovk[j, s, ESUM + HD : ESUM + HD + 1, :]
 
     def combine(j):
         arrive(ST_LO, j)
@@ -290,7 +306,7 @@
             delta = fin[j, s, 2:3, :]
             scaled = share * scale
             output = ovk[j, s, :HD, :] * share
-            grad_query = (ovk[j, s, 2 * HD :, :] - delta * ovk[j, s, HD : 2 * HD, :]) * scaled
+            grad_query = (ovk[j, s, ESUM : ESUM + HD, :] - delta * ovk[j, s, HD : 2 * HD, :]) * scaled
             if s == 1:
                 ovk[j, s, :HD, :] = output
                 ovk[j, s, HD : 2 * HD, :] = grad_query
@@ -305,86 +321,103 @@
             wt[HD:, ecols] = (flipped[HD:] * (-scaled * delta)).astype(bf16)
             wt[:HD, fcols] = jnp.zeros((HD, tok), bf16)
             wt[HD:, fcols] = (flipped[HD:] * scaled).astype(bf16)
-        for kt in (3, 4, 5, 0, 1, 2):
+        for kt in (3, 5, 0, 2, 4, 1):
             part = mm(ef[ring, rows(kt), :], wt[...], NT)
             if kt < 3:
                 dkv_own[j, kt] = part
             else:
                 dkv_out[j, kt - 3] = part.astype(bf16)
-            if kt == 5:
-                send(DKV, j)
+                send((DKV, DKV1, DKV2)[kt - 3], j)
+            if kt == 5 and heads > 1:
+                pl.when(j == heads - 1)(functools.partial(hand_back, heads - 2))
+            if kt == 2:
+                pl.when(j == heads - 1)(functools.partial(hand_back, heads - 1))
 
     def hand_back(j):
         arrive(DKV, j)
+        arrive(DKV2, j)
         for d, kind in ((0, DZ_HI), (2, DZ_LO)):
             dz_out[j, d // 2] = (dkv_own[j, d] + dkv_in[j, d].astype(f32)).astype(bf16)
             send(kind, j)
 
     def finish(j):
-        for kind in (OQ_LO, OQ_HI, DZ_LO, DZ_HI):
+        for kind in (OQ_LO, OQ_HI, DKV1, DZ_LO, DZ_HI):
             arrive(kind, j)
-        cols = pl.ds(pl.multiple_of(j * HD, HD), HD)
         both = ovk[j, 1, : 2 * HD, :] + oq_in[j, 0].astype(f32) + oq_in[j, 1].astype(f32)
         both = both.T
-        att_ref[:, cols] = both[:, :HD].astype(bf16)
-        gq_ref[:, cols] = both[:, HD:].astype(bf16)
+        result[j, 0] = both[:, :HD].astype(bf16)
+        result[j, 1] = both[:, HD:].astype(bf16)
         both = dkv_own[j, 1] + dkv_in[j, 1].astype(f32)
         both = both + dz_in[j, 0].astype(f32) + dz_in[j, 1].astype(f32)
-        gv_ref[:, cols] = both[:, :HD].astype(bf16)
-        gk_ref[:, cols] = both[:, HD:].astype(bf16)
+        result[j, 2] = both[:, HD:].astype(bf16)
+        result[j, 3] = both[:, :HD].astype(bf16)
+        for n in range(4):
+            output(j, n).start()
+
+    def output(j, n):
+        cols = pl.ds(pl.multiple_of(j * HD, HD), HD)
+        target = (att_ref, gq_ref, gk_ref, gv_ref)[n].at[:, cols]
+        return pltpu.make_async_copy(result.at[j, n], target, out_sem.at[j, n])
 
     def step(i, _):
-        @pl.when(i < heads)
-        def _():
-            prepare(i)
-
-        def inner(s, _):
+        pl.when(i < heads)(functools.partial(prepare, i))
+
+        def inner(turn, _):
+            s = lax.rem(2 * turn, 3)
+
             @pl.when(i < heads)
             def _():
                 forward(i, s)
 
-                @pl.when(s == 0)
+                @pl.when(turn == 0)
                 def _():
                     send(ST_HI, i)
 
-                @pl.when(s == 2)
+                @pl.when(turn == 1)
                 def _():
                     send(ST_LO, i)
 
-            @pl.when((s == 0) & (i + 1 < heads))
-            def _():
-                relay(i + 1)
-
-            @pl.when((s == 0) & (i >= 1) & (i <= heads))
-            def _():
-                combine(i - 1)
-
-            @pl.when((s == 1) & (i >= 2))
-            def _():
-                hand_back(i - 2)
-
+                @pl.when((turn == 0) & (i + 1 < heads))
+                def _():
+                    relay(i + 1)
+
+                @pl.when((turn == 0) & (i + AHEAD < heads))
+                def _():
+                    send_own(i + AHEAD, 0)
+
+                pl.when((turn == 1) & (i >= 2))(functools.partial(hand_back, i - 2))
+
+            pl.when((turn == 0) & (i >= 3))(functools.partial(finish, i - 3))
             return 0
 
         lax.fori_loop(0, 3, inner, 0)
-
-        @pl.when((i >= 1) & (i <= heads))
-        def _():
-            backward(i - 1)
-
-        @pl.when(i >= 2)
-        def _():
-            finish(i - 2)
-
+        pl.when(i < heads)(functools.partial(combine, i))
+        pl.when((i >= 1) & (i <= heads))(functools.partial(backward, i - 1))
         return 0
 
-    lax.fori_loop(0, heads + 2, step, 0)
+    lax.fori_loop(0, heads + 3, step, 0)
 
     def drain(j, _):
         for kind in range(KINDS):
             sent_off(kind, j)
+        for n in range(4):
+            output(j, n).wait()
         return 0
 
     lax.fori_loop(0, heads, drain, 0)
+
+
+def put(*refs):
+    sources, targets, (held, take_sem, give_sem) = refs[:4], refs[4:8], refs[8:]
+    takes = [pltpu.make_async_copy(sources[n], held.at[n], take_sem.at[n]) for n in range(4)]
+    gives = [pltpu.make_async_copy(held.at[n], targets[n], give_sem.at[n]) for n in range(4)]
+    for take in takes:
+        take.start()
+    for take, give in zip(takes, gives):
+        take.wait()
+        give.start()
+    for give in gives:
+        give.wait()
 
 
 def on_device(queries, keys, values, reward_grad, window_mask):
@@ -392,20 +425,21 @@
     heads = width // HD
     frames = lax.axis_size("tile") // (GH * GW)
     bf16, f32 = jnp.bfloat16, jnp.float32
-    hbm = pl.BlockSpec(memory_space=pl.ANY)
-    vmem = pl.BlockSpec(memory_space=pltpu.VMEM)
-    return pl.pallas_call(
+    hbm = pl.BlockSpec(memory_space=pltpu.MemorySpace.HBM)
+    results = pl.pallas_call(
         functools.partial(kernel, heads, tok, frames),
         out_shape=[jax.ShapeDtypeStruct((tok, width), bf16)] * 4,
         in_specs=[pl.BlockSpec(memory_space=pltpu.SMEM), hbm, hbm, hbm, hbm],
-        out_specs=[vmem] * 4,
+        out_specs=[hbm] * 4,
         scratch_shapes=[
             pltpu.VMEM((heads, 3 * tok, 2 * HD), bf16),
             pltpu.VMEM((heads, 6 * tok, 2 * HD), bf16),
-            pltpu.VMEM((2 * HD, 6 * tok), bf16),
+            pltpu.VMEM((ESUM, 6 * tok), bf16),
             pltpu.VMEM((6 * tok, tok), f32),
+            pltpu.VMEM((6 * tok, tok), f32),
+            pltpu.VMEM((8, tok), f32),
             pltpu.VMEM((2, 6 * tok, 6 * tok), bf16),
-            pltpu.VMEM((heads, 3, 3 * HD, tok), f32),
+            pltpu.VMEM((heads, 3, 2 * ESUM - HD, tok), f32),
             pltpu.VMEM((2 * HD, 6 * tok), bf16),
             pltpu.VMEM((heads, 3, 8, tok), f32),
             pltpu.VMEM((heads, 2, 8, tok), f32),
@@ -417,7 +451,9 @@
             pltpu.VMEM((heads, 3, tok, 2 * HD), bf16),
             pltpu.VMEM((heads, 2, tok, 2 * HD), bf16),
             pltpu.VMEM((heads, 2, tok, 2 * HD), bf16),
+            pltpu.VMEM((heads, 4, tok, HD), bf16),
             pltpu.SemaphoreType.DMA((2, heads)),
+            pltpu.SemaphoreType.DMA((heads, 4)),
             pltpu.SemaphoreType.DMA((KINDS, heads)),
             pltpu.SemaphoreType.DMA((KINDS, heads)),
         ],
@@ -425,6 +461,17 @@
             collective_id=0, has_side_effects=True, vmem_limit_bytes=60 * 1024 * 1024
         ),
     )(window_mask, queries, keys, values, reward_grad)
+    return pl.pallas_call(
+        put,
+        out_shape=[jax.ShapeDtypeStruct((tok, width), bf16)] * 4,
+        in_specs=[hbm] * 4,
+        out_specs=[hbm] * 4,
+        scratch_shapes=[
+            pltpu.VMEM((4, tok, width), bf16),
+            pltpu.SemaphoreType.DMA((4,)),
+            pltpu.SemaphoreType.DMA((4,)),
+        ],
+    )(*results)
 
 
 def solution(mesh):

time: 71.1 us -> 67 us (0.942)
  local copies, waits for them, and re-layouts: 4.68 us -> 0 us
    unnamed x10 -> x0, local copies, waits for them, and re-layouts: 4.68 us -> none
    pallas_call x1, Pallas kernels: 65.5 us -> 63.3 us  [on_device(): pl.pallas_call(functools.partial(kernel, heads, tok, frames), out_shape=[...]
    pallas_call x0 -> x1, Pallas kernels: none -> 2.09 us  [on_device(): pl.pallas_call(put, out_shape=[jax.ShapeDtypeStruct((tok, width), bf16)]...]
where the time goes in v2:
time: 67 us; the launch traced here: 66 us
  Pallas kernels  65.4 us (98%)
    pallas_call x1, Pallas kernels, on_device(): pl.pallas_call(functools.partial(kernel, heads, tok, frames), out_shape=[...  63.3 us
    pallas_call x1, Pallas kernels, on_device(): pl.pallas_call(put, out_shape=[jax.ShapeDtypeStruct((tok, width), bf16)]...  2.09 us

profile of v2, /device:TPU:1, one launch (start us, length us, event | category | flops | bytes accessed | tf_op | source)
XLA Modules:
  0.0 66.0 jit_solution(6291899330486100273)
XLA Ops:
  0.6 63.3 %shard_map.84 = (bf16[256,640]{1,0:T(8,128)(2,1)}, bf16[256,640]{1,0:T(8,128)(2,1)}, bf16[256,640]{1,0:T(8,128)(2,1)}, bf16[256,640]{1,0:T(8,128)(2,1)}) custom-call(s32[32,27]{1,0:T(8,128)} %mask_ref.1, bf16[256,640]{1,0:T(8,128)(2,1)} %q_hbm.1, bf16[256,640]{1,0:T(8,128)(2,1)} %k_hbm.1, bf16[256,640]{1,0:T(8,128)(2,1)} %v_hbm.1, bf16[256,640]{1,0:T(8,128)(2,1)} %g_hbm.1), custom_call_target="tpu_custom_call" | custom-call | tf_op jit(solution)/shard_map/pallas_call | solution.py:429
  64.0 2.1 %shard_map.85 = (bf16[256,640]{1,0:T(8,128)(2,1)}, bf16[256,640]{1,0:T(8,128)(2,1)}, bf16[256,640]{1,0:T(8,128)(2,1)}, bf16[256,640]{1,0:T(8,128)(2,1)}) custom-call(bf16[256,640]{1,0:T(8,128)(2,1)} %get-tuple-element.8.refs_0_, bf16[256,640]{1,0:T(8,128)(2,1)} %get-tuple-element.9.refs_1_, bf16[256,640]{1,0:T(8,128)(2,1)} %get-tuple-element.10.refs_2_, ...), custom_call_target="tpu_custom_call" | custom-call | tf_op jit(solution)/shard_map/pallas_call | solution.py:464

commit v3 on v2

--- a/solution.py
+++ b/solution.py
@@ -51,7 +51,7 @@
     kvt,
     scores,
     slopes,
-    limits,
+    first_top,
     ef,
     ovk,
     wt,
@@ -235,51 +235,65 @@
 
     relay(0)
 
-    def prepare(j):
+    def forward(j, hooks):
         for kind in (KVP, KVP + 1, KVP + 2, QD_LO, QD_HI):
             arrive(kind, j)
-        for kt in range(6):
-            kvt[: 2 * HD, rows(kt)] = kv[j, rows(kt), :].T
-
-    def forward(j, s):
         ring = lax.rem(j, 2)
-        qrows = pl.ds(pl.multiple_of(s * tok, tok), tok)
-        tile = me + (s - 1) * GW
-        near = row + s - 1
-        exists = jnp.where((near >= 0) & (near < GH), 1, 0)
-        tile = jnp.where(exists == 1, tile, me)
-        drops = []
-        for kt in range(6):
-            across = 1 if kt < 3 else 2 - 2 * column
-            flag = mask_ref[tile, kt % 3 * 9 + (2 - s) * 3 + across] * exists
-            drops.append((1 - flag).astype(f32))
-        query = qd[j, qrows, HD:]
-        grad = qd[j, qrows, :HD]
-        top = jnp.full((1, tok), NEG, f32)
-        for kt in range(6):
-            block = mm(kv[j, rows(kt), HD:], query, NT)
-            scores[rows(kt), :] = block
+        order = (0, 2, 1)
+
+        def dropped(s):
+            near = row + s - 1
+            exists = jnp.where((near >= 0) & (near < GH), 1, 0)
+            tile = jnp.where(exists == 1, me + (s - 1) * GW, me)
+            drops = []
+            for kt in range(6):
+                across = 1 if kt < 3 else 2 - 2 * column
+                flag = mask_ref[tile, kt % 3 * 9 + (2 - s) * 3 + across] * exists
+                drops.append((1 - flag).astype(f32))
+            return drops
+
+        def score(s, kt, drop, top, held):
+            block = mm(kv[j, rows(kt), HD:], qd[j, rows(s), HD:], NT)
+            scores[held][rows(kt), :] = block
+            slopes[held][rows(kt), :] = mm(kv[j, rows(kt), :HD], qd[j, rows(s), :HD], NT)
             peak = jnp.max(block, axis=0, keepdims=True)
-            top = jnp.maximum(top, peak * scale2 + drops[kt] * NEG)
-            slopes[rows(kt), :] = mm(kv[j, rows(kt), :HD], grad, NT)
-        for kt in range(6):
-            limits[kt : kt + 1, :] = top + drops[kt] * BIG
-        ecols = pl.ds(pl.multiple_of(s * 2 * tok, tok), tok)
-        fcols = pl.ds(pl.multiple_of((s * 2 + 1) * tok, tok), tok)
-
-        def weigh(kt, _):
-            krows = pl.ds(pl.multiple_of(kt * tok, tok), tok)
-            weight = jnp.exp2(scores[krows, :] * scale2 - limits[pl.ds(kt, 1), :])
-            ef[ring, krows, ecols] = weight.astype(bf16)
-            ef[ring, krows, fcols] = (weight * slopes[krows, :]).astype(bf16)
-            return 0
-
-        lax.fori_loop(0, 6, weigh, 0)
-        ovk[j, s, :ESUM, :] = mm(kvt[...], ef[ring, :, ecols])
-        ovk[j, s, ESUM:, :] = mm(kvt[HD:, :], ef[ring, :, fcols])
-        st[j, s, 0:1, :] = top
-        st[j, s, 1:2, :] = ovk[j, s, 2 * HD : 2 * HD + 1, :]
-        st[j, s, 2:3, :] = ovk[j, s, ESUM + HD : ESUM + HD + 1, :]
+            return jnp.maximum(top, peak * scale2 + drop * NEG)
+
+        empty = jnp.full((1, tok), NEG, f32)
+
+        @pl.when(me >= 0)
+        def _():
+            drops = dropped(order[0])
+            top = empty
+            for kt in range(6):
+                top = score(order[0], kt, drops[kt], top, 0)
+                kvt[: 2 * HD, rows(kt)] = kv[j, rows(kt), :].T
+            first_top[0:1, :] = top
+
+        drops = dropped(order[0])
+        top = first_top[0:1, :]
+        for turn, s in enumerate(order):
+            held = turn % 2
+            ecols, fcols = pl.ds(s * 2 * tok, tok), pl.ds((s * 2 + 1) * tok, tok)
+            later = empty
+            if turn < 2:
+                next_drops = dropped(order[turn + 1])
+            for kt in range(6):
+                limit = top + drops[kt] * BIG
+                weight = jnp.exp2(scores[held][rows(kt), :] * scale2 - limit)
+                ef[ring, rows(kt), ecols] = weight.astype(bf16)
+                ef[ring, rows(kt), fcols] = (weight * slopes[held][rows(kt), :]).astype(bf16)
+                if turn < 2:
+                    later = score(order[turn + 1], kt, next_drops[kt], later, 1 - held)
+            ovk[j, s, :ESUM, :] = mm(kvt[...], ef[ring, :, ecols])
+            ovk[j, s, ESUM:, :] = mm(kvt[HD:, :], ef[ring, :, fcols])
+            st[j, s, 0:1, :] = top
+            st[j, s, 1:2, :] = ovk[j, s, 2 * HD : 2 * HD + 1, :]
+            st[j, s, 2:3, :] = ovk[j, s, ESUM + HD : ESUM + HD + 1, :]
+            hooks[turn]()
+            top = later
+            if turn < 2:
+                drops = next_drops
 
     def combine(j):
         arrive(ST_LO, j)
@@ -297,7 +311,7 @@
         send(FIN_LO, j)
         send(FIN_HI, j)
 
-    def backward(j):
+    def backward(last, j):
         ring = lax.rem(j, 2)
         arrive(FIN_LO, j)
         arrive(FIN_HI, j)
@@ -313,7 +327,6 @@
             else:
                 oq_out[j, s // 2, :HD, :] = output.astype(bf16)
                 oq_out[j, s // 2, HD:, :] = grad_query.astype(bf16)
-                send(OQ_HI if s == 0 else OQ_LO, j)
             flipped = qd[j, rows(s), :].astype(f32).T
             ecols = pl.ds(s * 2 * tok, tok)
             fcols = pl.ds((s * 2 + 1) * tok, tok)
@@ -321,6 +334,9 @@
             wt[HD:, ecols] = (flipped[HD:] * (-scaled * delta)).astype(bf16)
             wt[:HD, fcols] = jnp.zeros((HD, tok), bf16)
             wt[HD:, fcols] = (flipped[HD:] * scaled).astype(bf16)
+        if last:
+            send(OQ_HI, j)
+            send(OQ_LO, j)
         for kt in (3, 5, 0, 2, 4, 1):
             part = mm(ef[ring, rows(kt), :], wt[...], NT)
             if kt < 3:
@@ -328,10 +344,11 @@
             else:
                 dkv_out[j, kt - 3] = part.astype(bf16)
                 send((DKV, DKV1, DKV2)[kt - 3], j)
-            if kt == 5 and heads > 1:
-                pl.when(j == heads - 1)(functools.partial(hand_back, heads - 2))
-            if kt == 2:
-                pl.when(j == heads - 1)(functools.partial(hand_back, heads - 1))
+            if last and kt == 2:
+                hand_back(heads - 1)
+        if not last:
+            send(OQ_HI, j)
+            send(OQ_LO, j)
 
     def hand_back(j):
         arrive(DKV, j)
@@ -360,51 +377,46 @@
         return pltpu.make_async_copy(result.at[j, n], target, out_sem.at[j, n])
 
     def step(i, _):
-        pl.when(i < heads)(functools.partial(prepare, i))
-
-        def inner(turn, _):
-            s = lax.rem(2 * turn, 3)
-
-            @pl.when(i < heads)
+        def first():
+            send(ST_HI, i)
+            pl.when(i + 1 < heads)(functools.partial(relay, i + 1))
+
+            @pl.when(i + AHEAD < heads)
             def _():
-                forward(i, s)
-
-                @pl.when(turn == 0)
-                def _():
-                    send(ST_HI, i)
-
-                @pl.when(turn == 1)
-                def _():
-                    send(ST_LO, i)
-
-                @pl.when((turn == 0) & (i + 1 < heads))
-                def _():
-                    relay(i + 1)
-
-                @pl.when((turn == 0) & (i + AHEAD < heads))
-                def _():
-                    send_own(i + AHEAD, 0)
-
-                pl.when((turn == 1) & (i >= 2))(functools.partial(hand_back, i - 2))
-
-            pl.when((turn == 0) & (i >= 3))(functools.partial(finish, i - 3))
-            return 0
-
-        lax.fori_loop(0, 3, inner, 0)
-        pl.when(i < heads)(functools.partial(combine, i))
-        pl.when((i >= 1) & (i <= heads))(functools.partial(backward, i - 1))
-        return 0
-
-    lax.fori_loop(0, heads + 3, step, 0)
+                send_own(i + AHEAD, 0)
+
+            pl.when(i >= 2)(functools.partial(hand_back, i - 2))
+
+        forward(i, (first, functools.partial(send, ST_LO, i), lambda: None))
+        pl.when(i >= 3)(functools.partial(finish, i - 3))
+        pl.when(i == heads - 1)(functools.partial(combine, i))
+        pl.when(i >= 1)(functools.partial(backward, False, i - 1))
+        pl.when(i < heads - 1)(functools.partial(combine, i))
+        return 0
+
+    lax.fori_loop(0, heads, step, 0)
+    if heads > 2:
+        finish(heads - 3)
+    if heads > 1:
+        hand_back(heads - 2)
+    backward(True, heads - 1)
+    if heads > 1:
+        finish(heads - 2)
 
     def drain(j, _):
         for kind in range(KINDS):
             sent_off(kind, j)
+        return 0
+
+    lax.fori_loop(0, heads, drain, 0)
+    finish(heads - 1)
+
+    def written(j, _):
         for n in range(4):
             output(j, n).wait()
         return 0
 
-    lax.fori_loop(0, heads, drain, 0)
+    lax.fori_loop(0, heads, written, 0)
 
 
 def put(*refs):
@@ -435,8 +447,8 @@
             pltpu.VMEM((heads, 3 * tok, 2 * HD), bf16),
             pltpu.VMEM((heads, 6 * tok, 2 * HD), bf16),
             pltpu.VMEM((ESUM, 6 * tok), bf16),
-            pltpu.VMEM((6 * tok, tok), f32),
-            pltpu.VMEM((6 * tok, tok), f32),
+            [pltpu.VMEM((6 * tok, tok), f32)] * 2,
+            [pltpu.VMEM((6 * tok, tok), f32)] * 2,
             pltpu.VMEM((8, tok), f32),
             pltpu.VMEM((2, 6 * tok, 6 * tok), bf16),
             pltpu.VMEM((heads, 3, 2 * ESUM - HD, tok), f32),

time: 67 us -> 62.6 us (0.934); the launches traced: 66 us -> 62.4 us
  Pallas kernels: 65.4 us -> 61.8 us
    pallas_call x1, Pallas kernels: 63.3 us -> 59.7 us  [on_device(): pl.pallas_call(functools.partial(kernel, heads, tok, frames), out_shape=[...]
where the time goes in v3:
time: 62.6 us; the launch traced here: 62.4 us
  Pallas kernels  61.8 us (99%)
  between operations  0.64 us (1%)
    pallas_call x1, Pallas kernels, on_device(): pl.pallas_call(functools.partial(kernel, heads, tok, frames), out_shape=[...  59.7 us
    pallas_call x1, Pallas kernels, on_device(): pl.pallas_call(put, out_shape=[jax.ShapeDtypeStruct((tok, width), bf16)]...  2.09 us

profile of v3, /device:TPU:1, one launch (start us, length us, event | category | flops | bytes accessed | tf_op | source)
XLA Modules:
  0.0 62.4 jit_solution(367626409746572976)
XLA Ops:
  0.6 59.7 %shard_map.84 = (bf16[256,640]{1,0:T(8,128)(2,1)}, bf16[256,640]{1,0:T(8,128)(2,1)}, bf16[256,640]{1,0:T(8,128)(2,1)}, bf16[256,640]{1,0:T(8,128)(2,1)}) custom-call(s32[32,27]{1,0:T(8,128)} %mask_ref.1, bf16[256,640]{1,0:T(8,128)(2,1)} %q_hbm.1, bf16[256,640]{1,0:T(8,128)(2,1)} %k_hbm.1, bf16[256,640]{1,0:T(8,128)(2,1)} %v_hbm.1, bf16[256,640]{1,0:T(8,128)(2,1)} %g_hbm.1), custom_call_target="tpu_custom_call" | custom-call | tf_op jit(solution)/shard_map/pallas_call | solution.py:441
  60.3 2.1 %shard_map.85 = (bf16[256,640]{1,0:T(8,128)(2,1)}, bf16[256,640]{1,0:T(8,128)(2,1)}, bf16[256,640]{1,0:T(8,128)(2,1)}, bf16[256,640]{1,0:T(8,128)(2,1)}) custom-call(bf16[256,640]{1,0:T(8,128)(2,1)} %get-tuple-element.8.refs_0_, bf16[256,640]{1,0:T(8,128)(2,1)} %get-tuple-element.9.refs_1_, bf16[256,640]{1,0:T(8,128)(2,1)} %get-tuple-element.10.refs_2_, ...), custom_call_target="tpu_custom_call" | custom-call | tf_op jit(solution)/shard_map/pallas_call | solution.py:476

commit v4 on v3

--- a/solution.py
+++ b/solution.py
@@ -167,6 +167,15 @@
         copy, sent, _ = copy_of(kind, j)
         guarded(sent, copy.wait_send)
 
+    barrier = pltpu.get_barrier_semaphore()
+
+    def greet(device):
+        pl.semaphore_signal(barrier, inc=1, device_id={"tile": device}, device_id_type=MESH)
+
+    greet(partner)
+    for there, device in ((has_ym, ym), (has_yp, yp), (has_zm, zm), (has_zp, zp)):
+        pl.when(there)(functools.partial(greet, device))
+
     def start_load(j, _):
         start = pl.multiple_of(j * HD, HD)
         for which, ref, buffer, lane in (
@@ -206,27 +215,23 @@
 
         return 0
 
-    barrier = pltpu.get_barrier_semaphore()
-
-    def greet(device):
-        pl.semaphore_signal(barrier, inc=1, device_id={"tile": device}, device_id_type=MESH)
-
-    greet(partner)
-    for there, device in ((has_ym, ym), (has_yp, yp), (has_zm, zm), (has_zp, zp)):
-        pl.when(there)(functools.partial(greet, device))
     lax.fori_loop(0, heads, blank, 0)
     peers = sum(jnp.where(there, 1, 0) for there in (has_ym, has_yp, has_zm, has_zp))
     pl.semaphore_wait(barrier, 1 + peers)
 
-    def send_own(j, _):
-        for which, buffer in ((1, kv), (0, qd)):
-            own = buffer.at[j, rows(1), :]
-            pltpu.make_async_copy(own, own, load_sem.at[which, j]).wait()
-            for kind in ((KV_LO, KV_HI, KVP + 1), (QD_LO, QD_HI))[1 - which]:
-                send(kind, j)
+    def send_own(which, j):
+        buffer = (qd, kv)[which]
+        own = buffer.at[j, rows(1), :]
+        pltpu.make_async_copy(own, own, load_sem.at[which, j]).wait()
+        for kind in ((QD_LO, QD_HI), (KV_LO, KV_HI, KVP + 1))[which]:
+            send(kind, j)
+
+    def open_with(j, _):
+        send_own(1, j)
+        send_own(0, j)
         return 0
 
-    lax.fori_loop(0, min(AHEAD, heads), send_own, 0)
+    lax.fori_loop(0, min(AHEAD, heads), open_with, 0)
 
     def relay(j):
         for kind, onward in ((KV_LO, KVP), (KV_HI, KVP + 2)):
@@ -337,6 +342,8 @@
         if last:
             send(OQ_HI, j)
             send(OQ_LO, j)
+        else:
+            pl.when(j == heads - 2)(functools.partial(combine, heads - 1))
         for kt in (3, 5, 0, 2, 4, 1):
             part = mm(ef[ring, rows(kt), :], wt[...], NT)
             if kt < 3:
@@ -346,9 +353,6 @@
                 send((DKV, DKV1, DKV2)[kt - 3], j)
             if last and kt == 2:
                 hand_back(heads - 1)
-        if not last:
-            send(OQ_HI, j)
-            send(OQ_LO, j)
 
     def hand_back(j):
         arrive(DKV, j)
@@ -380,28 +384,30 @@
         def first():
             send(ST_HI, i)
             pl.when(i + 1 < heads)(functools.partial(relay, i + 1))
-
-            @pl.when(i + AHEAD < heads)
-            def _():
-                send_own(i + AHEAD, 0)
-
+            pl.when(i + AHEAD < heads)(functools.partial(send_own, 1, i + AHEAD))
             pl.when(i >= 2)(functools.partial(hand_back, i - 2))
 
         forward(i, (first, functools.partial(send, ST_LO, i), lambda: None))
         pl.when(i >= 3)(functools.partial(finish, i - 3))
-        pl.when(i == heads - 1)(functools.partial(combine, i))
+        if heads == 1:
+            combine(i)
         pl.when(i >= 1)(functools.partial(backward, False, i - 1))
         pl.when(i < heads - 1)(functools.partial(combine, i))
+        pl.when(i + AHEAD < heads)(functools.partial(send_own, 0, i + AHEAD))
+
+        @pl.when(i >= 1)
+        def _():
+            send(OQ_HI, i - 1)
+            send(OQ_LO, i - 1)
+
         return 0
 
     lax.fori_loop(0, heads, step, 0)
-    if heads > 2:
-        finish(heads - 3)
     if heads > 1:
         hand_back(heads - 2)
     backward(True, heads - 1)
-    if heads > 1:
-        finish(heads - 2)
+    for j in range(max(heads - 3, 0), heads - 1):
+        finish(j)
 
     def drain(j, _):
         for kind in range(KINDS):

time: 62.6 us -> 61.7 us (0.986)
  Pallas kernels: 61.8 us -> 60.9 us
    pallas_call x1, Pallas kernels: 59.7 us -> 58.8 us  [on_device(): pl.pallas_call(functools.partial(kernel, heads, tok, frames), out_shape=[...]
where the time goes in v4:
time: 61.7 us; the launch traced here: 61.5 us
  Pallas kernels  60.9 us (99%)
  between operations  0.64 us (1%)
    pallas_call x1, Pallas kernels, on_device(): pl.pallas_call(functools.partial(kernel, heads, tok, frames), out_shape=[...  58.8 us
    pallas_call x1, Pallas kernels, on_device(): pl.pallas_call(put, out_shape=[jax.ShapeDtypeStruct((tok, width), bf16)]...  2.09 us

profile of v4, /device:TPU:1, one launch (start us, length us, event | category | flops | bytes accessed | tf_op | source)
XLA Modules:
  0.0 61.5 jit_solution(4386504691696632575)
XLA Ops:
  0.6 58.8 %shard_map.84 = (bf16[256,640]{1,0:T(8,128)(2,1)}, bf16[256,640]{1,0:T(8,128)(2,1)}, bf16[256,640]{1,0:T(8,128)(2,1)}, bf16[256,640]{1,0:T(8,128)(2,1)}) custom-call(s32[32,27]{1,0:T(8,128)} %mask_ref.1, bf16[256,640]{1,0:T(8,128)(2,1)} %q_hbm.1, bf16[256,640]{1,0:T(8,128)(2,1)} %k_hbm.1, bf16[256,640]{1,0:T(8,128)(2,1)} %v_hbm.1, bf16[256,640]{1,0:T(8,128)(2,1)} %g_hbm.1), custom_call_target="tpu_custom_call" | custom-call | tf_op jit(solution)/shard_map/pallas_call | solution.py:447
  59.4 2.1 %shard_map.85 = (bf16[256,640]{1,0:T(8,128)(2,1)}, bf16[256,640]{1,0:T(8,128)(2,1)}, bf16[256,640]{1,0:T(8,128)(2,1)}, bf16[256,640]{1,0:T(8,128)(2,1)}) custom-call(bf16[256,640]{1,0:T(8,128)(2,1)} %get-tuple-element.8.refs_0_, bf16[256,640]{1,0:T(8,128)(2,1)} %get-tuple-element.9.refs_1_, bf16[256,640]{1,0:T(8,128)(2,1)} %get-tuple-element.10.refs_2_, ...), custom_call_target="tpu_custom_call" | custom-call | tf_op jit(solution)/shard_map/pallas_call | solution.py:482
